TPU v7x, 768 devices: a whole 4x8x12 slice. The times are simulated.
768 devices in a mesh: gx: 24 (over x, z_hi, core), gy: 32 (over y, z_lo).
Axes of the slice: x: 4, y: 8, z: 12 (z_hi: 3, z_lo: 4; z = z_hi * 4 + z_lo), core: 2. Of those that a mesh axis runs over, the one named last changes fastest.
Arguments:
- spectrum: bfloat16 [384, 512, 1152], P('gx', 'gy'), may hold values from 0.099609375 to 1
- courant: float32 [2, 1152], replicated, may hold values from -0.45 to 0.45
- source: float32 [384, 512], P('gx', 'gy'), may hold values from 0.2 to 2
- wave_land: int32 [384, 512], P('gx', 'gy'), may hold values 0 or 1
- stokes_kernel: bfloat16 [1152, 128], replicated, may hold values from -0.1875 to 0.1875
- velocity: float32 [768, 2048, 128], P('gx', 'gy'), may hold values from -6 to 6
- coriolis: float32 [768, 2048], P('gx', 'gy'), may hold values from 0.5 to 1.5
- ocean_codes: int32 [768, 2048, 4], P('gx', 'gy'), may hold values from 0 to 8
- ocean_weights: float32 [768, 2048, 4], P('gx', 'gy'), may hold values from 0.2 to 2
- wave_codes: int32 [384, 512, 4], P('gx', 'gy'), may hold values from 0 to 23
- wave_weights: float32 [384, 512, 4], P('gx', 'gy'), may hold values from 0.2 to 2
Outputs:
- new_spectrum: bfloat16 [384, 512, 1152], P('gx', 'gy')
- new_velocity: float32 [768, 2048, 128], P('gx', 'gy')
- wave_current: float32 [2, 384, 512], P(None, 'gx', 'gy')
All inputs are finite; a program needn't handle non-finite values. No bound on the sum of `wave_land` on one device may be relied on, other than what follows from the above.
Results may differ from a plain program's by a relative error of at most 0.002.
Values may be sent and summed in bfloat16 or wider, within the bound.
A program may use at most 32 MiB of HBM per device.

v0:
```python
import jax
import jax.numpy as jnp
from jax import lax
from jax.sharding import PartitionSpec as P

NL = 64
K = 4
RX = 2
RY = 4


time_step = 0.5


def padded_2(value, sides, width):
    for axis, dim in sides:
        peers, length = (lax.axis_size(axis), value.shape[dim])
        up = [(i, (i + 1) % peers) for i in range(peers)]
        down = [(j, i) for i, j in up]
        last = lax.slice_in_dim(value, length - width, length, axis=dim)
        leading = lax.slice_in_dim(value, 0, width, axis=dim)
        before = lax.ppermute(last, axis, up)
        after = lax.ppermute(leading, axis, down)
        value = jnp.concatenate([before, value, after], axis=dim)
    return value


def clear_edges(padded, dim, width):
    index = lax.axis_index("gy")
    count = lax.axis_size("gy")
    length = padded.shape[dim]
    position = lax.broadcasted_iota(jnp.int32, (length,), 0)
    dropped = (position < width) & (index == 0) | (position >= length - width) & (
        index == count - 1
    )
    shape = [1] * padded.ndim
    shape[dim] = length
    return jnp.where(dropped.reshape(shape), jnp.zeros((), padded.dtype), padded)


def stokes_on(profiles_flat, codes, normed, wave_cols, rim):
    rows, cols = (codes.shape[0], codes.shape[1])
    ocean_x = lax.broadcasted_iota(jnp.int32, (rows, cols), 0)
    ocean_y = lax.broadcasted_iota(jnp.int32, (rows, cols), 1)
    stokes = jnp.zeros((rows, cols, profiles_flat.shape[1]), jnp.float32)
    for entry in range(K):
        code = codes[:, :, entry]
        slot = (
            (ocean_x // RX + code // 3 - 1 + rim) * (wave_cols + 2 * rim)
            + ocean_y // RY
            + code % 3
            - 1
            + rim
        )
        stokes = stokes + normed[:, :, entry : entry + 1] * jnp.take(
            profiles_flat, slot, axis=0
        ).astype(jnp.float32)
    return stokes


def stencil(along_x, along_y, coriolis_part, stokes):
    dvdx = (8.0 * (along_x[3:-1] - along_x[1:-3]) - (along_x[4:] - along_x[:-4])) / 12.0
    dudy = (8.0 * (along_y[:, 3:-1] - along_y[:, 1:-3]) - (along_y[:, 4:] - along_y[:, :-4])) / 12.0
    absolute = coriolis_part[:, :, None] + dvdx - dudy
    return jnp.concatenate([absolute * stokes[:, :, NL:], -absolute * stokes[:, :, :NL]], axis=-1)


def shards(
    spectrum,
    courant,
    source,
    wave_land,
    stokes_kernel,
    velocity,
    coriolis,
    ocean_codes,
    ocean_weights,
    wave_codes,
    wave_weights,
):
    wave_rows, wave_cols, bins = spectrum.shape
    ocean_rows, ocean_cols, levels_two = velocity.shape
    padded = padded_2(spectrum, (("gx", 0), ("gy", 1)), 1)
    padded = clear_edges(padded, 1, 1).astype(jnp.float32)
    center = padded[1:-1, 1:-1]
    speed_x = courant[0]
    speed_y = courant[1]
    advected = (
        center
        - jnp.maximum(speed_x, 0.0) * (center - padded[:-2, 1:-1])
        - jnp.maximum(-speed_x, 0.0) * (center - padded[2:, 1:-1])
        - jnp.maximum(speed_y, 0.0) * (center - padded[1:-1, :-2])
        - jnp.maximum(-speed_y, 0.0) * (center - padded[1:-1, 2:])
    )
    land_cells = wave_land.astype(jnp.float32)[:, :, None]
    source_cells = source[:, :, None]
    new_spectrum = (
        land_cells * (advected + 0.2 * source_cells * advected - 0.1 * advected * advected)
    ).astype(jnp.bfloat16)
    profiles = jnp.dot(
        new_spectrum.reshape(-1, bins), stokes_kernel, preferred_element_type=jnp.float32
    )
    profiles = profiles.astype(jnp.bfloat16).reshape(wave_rows, wave_cols, levels_two)
    ocean_normed = ocean_weights / jnp.sum(ocean_weights, axis=-1, keepdims=True)
    profiles_padded = padded_2(profiles, (("gx", 0), ("gy", 1)), 1)
    profiles_flat = clear_edges(profiles_padded, 1, 1).reshape(-1, levels_two)
    stokes = stokes_on(profiles_flat, ocean_codes, ocean_normed, wave_cols, 1)

    def tendency(state):
        wide = padded_2(state.astype(jnp.bfloat16), (("gx", 0), ("gy", 1)), 2).astype(state.dtype)
        wide = clear_edges(wide, 1, 2)
        along_x = wide[:, 2:-2, NL:]
        along_y = wide[2:-2, :, :NL]
        return stencil(along_x, along_y, coriolis, stokes)

    first = tendency(velocity)
    middle = velocity + time_step * first
    second = tendency(middle)
    new_velocity = velocity + 0.5 * time_step * (first + second)
    means = jnp.stack(
        [jnp.mean(new_velocity[:, :, :NL], axis=-1), jnp.mean(new_velocity[:, :, NL:], axis=-1)],
        axis=0,
    )
    means_padded = padded_2(means, (("gx", 1), ("gy", 2)), 1)
    means_flat = clear_edges(means_padded, 2, 1).reshape(2, -1)
    grid_x = lax.broadcasted_iota(jnp.int32, (wave_rows, wave_cols), 0)
    grid_y = lax.broadcasted_iota(jnp.int32, (wave_rows, wave_cols), 1)
    wave_normed = wave_weights / jnp.sum(wave_weights, axis=-1, keepdims=True)
    current = jnp.zeros((2, wave_rows, wave_cols), jnp.float32)
    for entry in range(K):
        code = wave_codes[:, :, entry]
        slot = (RX * grid_x + code // (RY + 2)) * (ocean_cols + 2) + RY * grid_y + code % (RY + 2)
        current = current + wave_normed[None, :, :, entry] * jnp.take(means_flat, slot, axis=1)
    return (new_spectrum, new_velocity, current)


def solution(mesh):
    return jax.shard_map(
        shards,
        mesh=mesh,
        in_specs=(
            P("gx", "gy", None),
            P(),
            P("gx", "gy"),
            P("gx", "gy"),
            P(),
            P("gx", "gy", None),
            P("gx", "gy"),
            P("gx", "gy", None),
            P("gx", "gy", None),
            P("gx", "gy", None),
            P("gx", "gy", None),
        ),
        out_specs=(P("gx", "gy", None), P("gx", "gy", None), P(None, "gx", "gy")),
        check_vma=False,
    )
```

profile of v0, /device:TPU:216, one launch (start us, length us, event | category | flops | bytes accessed | tf_op | source)
XLA Modules:
  0.0 184.0 jit_solution(11563120991012337303)
XLA Ops:
  0.7 0.8 fusion.84
  1.5 2.1 %collective-permute-start = (bf16[1,16,1152]{2,1,0:T(8,128)(2,1)S(1)}, bf16[1,16,1152]{2,1,0:T(8,128)(2,1)S(1)}, u32[]{:S(2)}, u32[]{:S(2)}) collective-permute-start(bf16[1,16,1152]{2,1,0:T(8,128)(2,1)S(1)} %get-tuple-element.38), channel_id=1, source_target_pairs={{0,32},{32,64},{64,96},{96,128},{128,160},{160,192},{192,224},{224... | collective-permute-start | bytes 110600 | tf_op jit(solution)/shard_map/ppermute | solution.py:22
  3.6 13.6 %collective-permute-start.1 = (bf16[1,16,1152]{2,1,0:T(8,128)(2,1)S(1)}, bf16[1,16,1152]{2,1,0:T(8,128)(2,1)S(1)}, u32[]{:S(2)}, u32[]{:S(2)}) collective-permute-start(bf16[1,16,1152]{2,1,0:T(8,128)(2,1)S(1)} %get-tuple-element.37), channel_id=1, source_target_pairs={{32,0},{64,32},{96,64},{128,96},{160,128},{192,160},{224,192},{256... | collective-permute-start | bytes 110600 | tf_op jit(solution)/shard_map/ppermute | solution.py:23
  17.3 1.3 convert_element_type.39
  18.6 1.9 %collective-permute-start.4 = (bf16[2,64,128]{2,1,0:T(8,128)(2,1)S(1)}, bf16[2,64,128]{2,1,0:T(8,128)(2,1)S(1)}, u32[]{:S(2)}, u32[]{:S(2)}) collective-permute-start(bf16[2,64,128]{2,1,0:T(8,128)(2,1)S(1)} %get-tuple-element.41), channel_id=1, source_target_pairs={{0,32},{32,64},{64,96},{96,128},{128,160},{160,192},{192,224},{224... | collective-permute-start | bytes 98312 | tf_op jit(solution)/shard_map/ppermute | solution.py:22
  20.5 9.7 %collective-permute-start.5 = (bf16[2,64,128]{2,1,0:T(8,128)(2,1)S(1)}, bf16[2,64,128]{2,1,0:T(8,128)(2,1)S(1)}, u32[]{:S(2)}, u32[]{:S(2)}) collective-permute-start(bf16[2,64,128]{2,1,0:T(8,128)(2,1)S(1)} %get-tuple-element.42), channel_id=1, source_target_pairs={{32,0},{64,32},{96,64},{128,96},{160,128},{192,160},{224,192},{256... | collective-permute-start | bytes 98312 | tf_op jit(solution)/shard_map/ppermute | solution.py:23
  30.4 1.3 fusion.88
  32.4 0.7 fusion.91
  33.4 4.7 %collective-permute-start.2 = (bf16[18,1,1152]{2,1,0:T(2,128)(2,1)S(1)}, bf16[18,1,1152]{2,1,0:T(2,128)(2,1)S(1)}, u32[]{:S(2)}, u32[]{:S(2)}) collective-permute-start(bf16[18,1,1152]{2,1,0:T(2,128)(2,1)S(1)} %get-tuple-element.31), channel_id=1, source_target_pairs={{0,1},{1,2},{2,3},{3,4},{4,5},{5,6},{6,7},{7,8},{8,9},{9,10},{10,1... | collective-permute-start | bytes 124424 | tf_op jit(solution)/shard_map/ppermute | solution.py:22
  38.1 1.9 %collective-permute-start.3 = (bf16[18,1,1152]{2,1,0:T(2,128)(2,1)S(1)}, bf16[18,1,1152]{2,1,0:T(2,128)(2,1)S(1)}, u32[]{:S(2)}, u32[]{:S(2)}) collective-permute-start(bf16[18,1,1152]{2,1,0:T(2,128)(2,1)S(1)} %get-tuple-element.32), channel_id=1, source_target_pairs={{1,0},{2,1},{3,2},{4,3},{5,4},{6,5},{7,6},{8,7},{9,8},{10,9},{11,1... | collective-permute-start | bytes 124424 | tf_op jit(solution)/shard_map/ppermute | solution.py:23
  40.2 8.2 %collective-permute-done.3 = bf16[18,1,1152]{2,1,0:T(2,128)(2,1)S(1)} collective-permute-done((bf16[18,1,1152]{2,1,0:T(2,128)(2,1)S(1)}, bf16[18,1,1152]{2,1,0:T(2,128)(2,1)S(1)}, u32[]{:S(2)}, u32[]{:S(2)}) %collective-permute-start.3) | collective-permute-done | bytes 41504 | tf_op jit(solution)/shard_map/ppermute | solution.py:23
  48.8 0.9 fusion.2
  50.1 1.9 %collective-permute-start.8 = (bf16[1,16,128]{2,1,0:T(8,128)(2,1)S(1)}, bf16[1,16,128]{2,1,0:T(8,128)(2,1)S(1)}, u32[]{:S(2)}, u32[]{:S(2)}) collective-permute-start(bf16[1,16,128]{2,1,0:T(8,128)(2,1)S(1)} %get-tuple-element.54), channel_id=1, source_target_pairs={{0,32},{32,64},{64,96},{96,128},{128,160},{160,192},{192,224},{224... | collective-permute-start | bytes 12296 | tf_op jit(solution)/shard_map/ppermute | solution.py:22
  52.0 9.7 %collective-permute-start.9 = (bf16[1,16,128]{2,1,0:T(8,128)(2,1)S(1)}, bf16[1,16,128]{2,1,0:T(8,128)(2,1)S(1)}, u32[]{:S(2)}, u32[]{:S(2)}) collective-permute-start(bf16[1,16,128]{2,1,0:T(8,128)(2,1)S(1)} %get-tuple-element.55), channel_id=1, source_target_pairs={{32,0},{64,32},{96,64},{128,96},{160,128},{192,160},{224,192},{256... | collective-permute-start | bytes 12296 | tf_op jit(solution)/shard_map/ppermute | solution.py:23
  61.8 1.9 %collective-permute-start.6 = (bf16[36,2,128]{2,1,0:T(2,128)(2,1)S(1)}, bf16[36,2,128]{2,1,0:T(2,128)(2,1)S(1)}, u32[]{:S(2)}, u32[]{:S(2)}) collective-permute-start(bf16[36,2,128]{2,1,0:T(2,128)(2,1)S(1)} %get-tuple-element.35), channel_id=1, source_target_pairs={{0,1},{1,2},{2,3},{3,4},{4,5},{5,6},{6,7},{7,8},{8,9},{9,10},{10,1... | collective-permute-start | bytes 55304 | tf_op jit(solution)/shard_map/ppermute | solution.py:22
  63.7 3.9 %collective-permute-start.7 = (bf16[36,2,128]{2,1,0:T(2,128)(2,1)S(1)}, bf16[36,2,128]{2,1,0:T(2,128)(2,1)S(1)}, u32[]{:S(2)}, u32[]{:S(2)}) collective-permute-start(bf16[36,2,128]{2,1,0:T(2,128)(2,1)S(1)} %get-tuple-element.36), channel_id=1, source_target_pairs={{1,0},{2,1},{3,2},{4,3},{5,4},{6,5},{7,6},{8,7},{9,8},{10,9},{11,1... | collective-permute-start | bytes 55304 | tf_op jit(solution)/shard_map/ppermute | solution.py:23
  67.7 5.8 %collective-permute-start.10 = (bf16[18,1,128]{2,1,0:T(2,128)(2,1)S(1)}, bf16[18,1,128]{2,1,0:T(2,128)(2,1)S(1)}, u32[]{:S(2)}, u32[]{:S(2)}) collective-permute-start(bf16[18,1,128]{2,1,0:T(2,128)(2,1)S(1)} %get-tuple-element.43), channel_id=1, source_target_pairs={{0,1},{1,2},{2,3},{3,4},{4,5},{5,6},{6,7},{7,8},{8,9},{9,10},{10,1... | collective-permute-start | bytes 13832 | tf_op jit(solution)/shard_map/ppermute | solution.py:22
  73.5 1.9 %collective-permute-start.11 = (bf16[18,1,128]{2,1,0:T(2,128)(2,1)S(1)}, bf16[18,1,128]{2,1,0:T(2,128)(2,1)S(1)}, u32[]{:S(2)}, u32[]{:S(2)}) collective-permute-start(bf16[18,1,128]{2,1,0:T(2,128)(2,1)S(1)} %get-tuple-element.44), channel_id=1, source_target_pairs={{1,0},{2,1},{3,2},{4,3},{5,4},{6,5},{7,6},{8,7},{9,8},{10,9},{11,1... | collective-permute-start | bytes 13832 | tf_op jit(solution)/shard_map/ppermute | solution.py:23
  75.8 7.2 %collective-permute-done.11 = bf16[18,1,128]{2,1,0:T(2,128)(2,1)S(1)} collective-permute-done((bf16[18,1,128]{2,1,0:T(2,128)(2,1)S(1)}, bf16[18,1,128]{2,1,0:T(2,128)(2,1)S(1)}, u32[]{:S(2)}, u32[]{:S(2)}) %collective-permute-start.11) | collective-permute-done | bytes 4640 | tf_op jit(solution)/shard_map/ppermute | solution.py:23
  83.2 6.2 %gather_fusion.1 = bf16[2048,128]{1,0:T(8,128)(2,1)S(1)} fusion(bf16[324,128]{1,0:T(8,128)(2,1)S(1)} %broadcast_select_fusion.1, s32[2048]{0:T(1024)S(1)} %broadcast_clamp_fusion.2), kind=kCustom, calls=%fused_computation.2.clone | custom fusion | bytes 1056768 | tf_op jit(solution)/shard_map/jit(_take)/gather | solution.py:55
  89.4 8.0 %gather_fusion.2 = bf16[2048,128]{1,0:T(8,128)(2,1)} fusion(bf16[324,128]{1,0:T(8,128)(2,1)S(1)} %broadcast_select_fusion.1, s32[2048]{0:T(1024)S(1)} %broadcast_clamp_fusion.1), kind=kCustom, calls=%fused_computation.3.clone | custom fusion | bytes 1056768 | tf_op jit(solution)/shard_map/jit(_take)/gather | solution.py:55
  97.4 8.0 %gather_fusion = bf16[2048,128]{1,0:T(8,128)(2,1)} fusion(bf16[324,128]{1,0:T(8,128)(2,1)S(1)} %broadcast_select_fusion.1, s32[2048]{0:T(1024)S(1)} %broadcast_clamp_fusion.3), kind=kCustom, calls=%fused_computation.clone | custom fusion | bytes 1056768 | tf_op jit(solution)/shard_map/jit(_take)/gather | solution.py:55
  105.4 8.0 %gather_fusion.3 = bf16[2048,128]{1,0:T(8,128)(2,1)} fusion(bf16[324,128]{1,0:T(8,128)(2,1)S(1)} %broadcast_select_fusion.1, s32[2048]{0:T(1024)S(1)} %broadcast_clamp_fusion), kind=kCustom, calls=%fused_computation.4.clone | custom fusion | bytes 1056768 | tf_op jit(solution)/shard_map/jit(_take)/gather | solution.py:55
  113.5 5.5 %multiply_add_fusion.1 = f32[32,64,128]{2,1,0:T(8,128)S(1)} fusion(bf16[32,64,128]{2,1,0:T(8,128)(2,1)} %bitcast.228, bf16[32,64,128]{2,1,0:T(8,128)(2,1)} %bitcast.226, bf16[32,64,128]{2,1,0:T(8,128)(2,1)S(1)} %bitcast.225, bf16[32,64,128]{2,1,0:T(8,128)(2,1)} %bitcast.227, f32[32,64]{1,0:T(8,128)S(1)} %bitcast.236, f32[32,64]{1,0:T(8,128)S(1)} %bitcast.237, ...), kind=kLoop, calls=%fused_computation.61 | loop fusion | flops 3932160 | bytes 3186688 | tf_op jit(solution)/shard_map/add | solution.py:55
  119.0 2.0 %slice_multiply_fusion.1 = (f32[32,64,64]{2,1,0:T(8,128)S(1)}, f32[32,64,64]{2,1,0:T(8,128)S(1)}) fusion(f32[32,64,128]{2,1,0:T(8,128)S(1)} %multiply_add_fusion.1, f32[36,68,128]{2,1,0:T(8,128)S(1)} %convert_select_fusion.1, f32[32,64]{1,0:T(8,128)S(1)} %copy-done.10), kind=kLoop, calls=%fused_computation.65 | loop fusion | flops 1703936 | bytes 5775360 | tf_op jit(solution)/shard_map/mul | solution.py:65
  121.2 0.8 copy-done.4
  122.0 0.6 copy-done.1
  123.0 1.9 %collective-permute-start.12 = (bf16[2,64,128]{2,1,0:T(8,128)(2,1)S(1)}, bf16[2,64,128]{2,1,0:T(8,128)(2,1)S(1)}, u32[]{:S(2)}, u32[]{:S(2)}) collective-permute-start(bf16[2,64,128]{2,1,0:T(8,128)(2,1)S(1)} %get-tuple-element.39), channel_id=1, source_target_pairs={{0,32},{32,64},{64,96},{96,128},{128,160},{160,192},{192,224},{224... | collective-permute-start | bytes 98312 | tf_op jit(solution)/shard_map/ppermute | solution.py:22
  124.9 9.7 %collective-permute-start.13 = (bf16[2,64,128]{2,1,0:T(8,128)(2,1)S(1)}, bf16[2,64,128]{2,1,0:T(8,128)(2,1)S(1)}, u32[]{:S(2)}, u32[]{:S(2)}) collective-permute-start(bf16[2,64,128]{2,1,0:T(8,128)(2,1)S(1)} %get-tuple-element.40), channel_id=1, source_target_pairs={{32,0},{64,32},{96,64},{128,96},{160,128},{192,160},{224,192},{256... | collective-permute-start | bytes 98312 | tf_op jit(solution)/shard_map/ppermute | solution.py:23
  134.8 1.4 collective-permute-done.13
  136.2 1.9 %collective-permute-start.14 = (bf16[36,2,128]{2,1,0:T(2,128)(2,1)S(1)}, bf16[36,2,128]{2,1,0:T(2,128)(2,1)S(1)}, u32[]{:S(2)}, u32[]{:S(2)}) collective-permute-start(bf16[36,2,128]{2,1,0:T(2,128)(2,1)S(1)} %get-tuple-element.33), channel_id=1, source_target_pairs={{0,1},{1,2},{2,3},{3,4},{4,5},{5,6},{6,7},{7,8},{8,9},{9,10},{10,1... | collective-permute-start | bytes 55304 | tf_op jit(solution)/shard_map/ppermute | solution.py:22
  138.1 4.1 %collective-permute-start.15 = (bf16[36,2,128]{2,1,0:T(2,128)(2,1)S(1)}, bf16[36,2,128]{2,1,0:T(2,128)(2,1)S(1)}, u32[]{:S(2)}, u32[]{:S(2)}) collective-permute-start(bf16[36,2,128]{2,1,0:T(2,128)(2,1)S(1)} %get-tuple-element.34), channel_id=1, source_target_pairs={{1,0},{2,1},{3,2},{4,3},{5,4},{6,5},{7,6},{8,7},{9,8},{10,9},{11,1... | collective-permute-start | bytes 55304 | tf_op jit(solution)/shard_map/ppermute | solution.py:23
  142.4 5.3 %collective-permute-done.15 = bf16[36,2,128]{2,1,0:T(2,128)(2,1)S(1)} collective-permute-done((bf16[36,2,128]{2,1,0:T(2,128)(2,1)S(1)}, bf16[36,2,128]{2,1,0:T(2,128)(2,1)S(1)}, u32[]{:S(2)}, u32[]{:S(2)}) %collective-permute-start.15) | collective-permute-done | bytes 18464 | tf_op jit(solution)/shard_map/ppermute | solution.py:23
  148.0 2.0 %slice_multiply_fusion = (f32[32,64,64]{2,1,0:T(8,128)S(1)}, f32[32,64,64]{2,1,0:T(8,128)S(1)}) fusion(f32[32,64,128]{2,1,0:T(8,128)S(1)} %multiply_add_fusion.1, f32[36,68,128]{2,1,0:T(8,128)S(1)} %convert_select_fusion, f32[32,64]{1,0:T(8,128)S(1)} %copy-done.10), kind=kLoop, calls=%fused_computation.64 | loop fusion | flops 1703936 | bytes 5775360 | tf_op jit(solution)/shard_map/mul | solution.py:65
  150.2 1.0 copy-done.2
  151.5 0.7 fusion.28
  152.3 0.9 slice_reduce_fusion.1
  153.2 1.9 %collective-permute-start.16 = (f32[2,1,64]{2,1,0:T(1,128)S(1)}, f32[2,1,64]{2,1,0:T(1,128)S(1)}, u32[]{:S(2)}, u32[]{:S(2)}) collective-permute-start(f32[2,1,64]{2,1,0:T(1,128)S(1)} %get-tuple-element.67), channel_id=1, source_target_pairs={{0,32},{32,64},{64,96},{96,128},{128,160},{160,192},{192,224},{224... | collective-permute-start | bytes 1544 | tf_op jit(solution)/shard_map/ppermute | solution.py:22
  155.1 9.7 %collective-permute-start.17 = (f32[2,1,64]{2,1,0:T(1,128)S(1)}, f32[2,1,64]{2,1,0:T(1,128)S(1)}, u32[]{:S(2)}, u32[]{:S(2)}) collective-permute-start(f32[2,1,64]{2,1,0:T(1,128)S(1)} %get-tuple-element.68), channel_id=1, source_target_pairs={{32,0},{64,32},{96,64},{128,96},{160,128},{192,160},{224,192},{256... | collective-permute-start | bytes 1544 | tf_op jit(solution)/shard_map/ppermute | solution.py:23
  164.8 1.3 collective-permute-done.17
  166.2 1.9 %collective-permute-start.18 = (f32[2,34,1]{2,1,0:T(8,128)S(1)}, f32[2,34,1]{2,1,0:T(8,128)S(1)}, u32[]{:S(2)}, u32[]{:S(2)}) collective-permute-start(f32[2,34,1]{2,1,0:T(8,128)S(1)} %get-tuple-element.56), channel_id=1, source_target_pairs={{0,1},{1,2},{2,3},{3,4},{4,5},{5,6},{6,7},{7,8},{8,9},{9,10},{10,1... | collective-permute-start | bytes 824 | tf_op jit(solution)/shard_map/ppermute | solution.py:22
  168.1 3.9 %collective-permute-start.19 = (f32[2,34,1]{2,1,0:T(8,128)S(1)}, f32[2,34,1]{2,1,0:T(8,128)S(1)}, u32[]{:S(2)}, u32[]{:S(2)}) collective-permute-start(f32[2,34,1]{2,1,0:T(8,128)S(1)} %get-tuple-element.57), channel_id=1, source_target_pairs={{1,0},{2,1},{3,2},{4,3},{5,4},{6,5},{7,6},{8,7},{9,8},{10,9},{11,1... | collective-permute-start | bytes 824 | tf_op jit(solution)/shard_map/ppermute | solution.py:23
  172.2 5.7 %collective-permute-done.19 = f32[2,34,1]{2,1,0:T(8,128)S(1)} collective-permute-done((f32[2,34,1]{2,1,0:T(8,128)S(1)}, f32[2,34,1]{2,1,0:T(8,128)S(1)}, u32[]{:S(2)}, u32[]{:S(2)}) %collective-permute-start.19) | collective-permute-done | bytes 304 | tf_op jit(solution)/shard_map/ppermute | solution.py:23
  178.5 1.2 broadcast_select_fusion
  179.7 0.7 gather_fusion.4
  180.6 0.8 gather_fusion.5
  181.5 0.8 gather_fusion.6
  182.4 0.8 gather_fusion.7
  (116 shorter events, 6.4 us)
Async XLA Ops:
  0.6 49.2 %copy-start = (bf16[1152,128]{1,0:T(8,128)(2,1)S(1)}, bf16[1152,128]{1,0:T(8,128)(2,1)}, u32[]{:S(2)}) copy-start(bf16[1152,128]{1,0:T(8,128)(2,1)} %param.19) | copy-start | bytes 884740
  0.6 29.6 %copy-start.13 = (f32[2,1152]{1,0:T(2,128)S(1)}, f32[2,1152]{1,0:T(2,128)}, u32[]{:S(2)}) copy-start(f32[2,1152]{1,0:T(2,128)} %param.16) | copy-start | bytes 27652
  0.7 29.7 %copy-start.14 = (f32[16,16]{1,0:T(8,128)S(1)}, f32[16,16]{1,0:T(8,128)}, u32[]{:S(2)}) copy-start(f32[16,16]{1,0:T(8,128)} %param.17) | copy-start | bytes 3076
  0.7 29.7 %copy-start.11 = (s32[32,64,4]{1,2,0:T(4,128)S(1)}, s32[32,64,4]{1,2,0:T(4,128)}, u32[]{:S(2)}) copy-start(s32[32,64,4]{1,2,0:T(4,128)} %param.22) | copy-start | bytes 98308
  1.5 30.6 %copy-start.8 = (f32[32,64,4]{1,2,0:T(4,128)S(1)}, f32[32,64,4]{1,2,0:T(4,128)}, u32[]{:S(2)}) copy-start(f32[32,64,4]{1,2,0:T(4,128)} %param.23) | copy-start | bytes 98308
  1.5 31.6 %collective-permute-start = (bf16[1,16,1152]{2,1,0:T(8,128)(2,1)S(1)}, bf16[1,16,1152]{2,1,0:T(8,128)(2,1)S(1)}, u32[]{:S(2)}, u32[]{:S(2)}) collective-permute-start(bf16[1,16,1152]{2,1,0:T(8,128)(2,1)S(1)} %get-tuple-element.38), channel_id=1, source_target_pairs={{0,32},{32,64},{64,96},{96,128},{128,160},{160,192},{192,224},{224... | collective-permute-start | bytes 110600 | tf_op jit(solution)/shard_map/ppermute | solution.py:22
  3.6 28.7 %copy-start.9 = (f32[16,16,4]{1,2,0:T(4,128)S(1)}, f32[16,16,4]{1,2,0:T(4,128)}, u32[]{:S(2)}) copy-start(f32[16,16,4]{1,2,0:T(4,128)} %param.25) | copy-start | bytes 12292
  3.6 28.8 %copy-start.12 = (s32[16,16,4]{1,2,0:T(4,128)S(1)}, s32[16,16,4]{1,2,0:T(4,128)}, u32[]{:S(2)}) copy-start(s32[16,16,4]{1,2,0:T(4,128)} %param.24) | copy-start | bytes 12292
  3.6 29.6 %copy-start.7 = (bf16[16,16,1152]{2,1,0:T(8,128)(2,1)S(1)}, bf16[16,16,1152]{2,1,0:T(8,128)(2,1)}, u32[]{:S(2)}) copy-start(bf16[16,16,1152]{2,1,0:T(8,128)(2,1)} %param.15) | copy-start | bytes 1769476
  3.6 29.7 %collective-permute-start.1 = (bf16[1,16,1152]{2,1,0:T(8,128)(2,1)S(1)}, bf16[1,16,1152]{2,1,0:T(8,128)(2,1)S(1)}, u32[]{:S(2)}, u32[]{:S(2)}) collective-permute-start(bf16[1,16,1152]{2,1,0:T(8,128)(2,1)S(1)} %get-tuple-element.37), channel_id=1, source_target_pairs={{32,0},{64,32},{96,64},{128,96},{160,128},{192,160},{224,192},{256... | collective-permute-start | bytes 110600 | tf_op jit(solution)/shard_map/ppermute | solution.py:23
  18.6 43.1 %collective-permute-start.4 = (bf16[2,64,128]{2,1,0:T(8,128)(2,1)S(1)}, bf16[2,64,128]{2,1,0:T(8,128)(2,1)S(1)}, u32[]{:S(2)}, u32[]{:S(2)}) collective-permute-start(bf16[2,64,128]{2,1,0:T(8,128)(2,1)S(1)} %get-tuple-element.41), channel_id=1, source_target_pairs={{0,32},{32,64},{64,96},{96,128},{128,160},{160,192},{192,224},{224... | collective-permute-start | bytes 98312 | tf_op jit(solution)/shard_map/ppermute | solution.py:22
  20.5 41.2 %collective-permute-start.5 = (bf16[2,64,128]{2,1,0:T(8,128)(2,1)S(1)}, bf16[2,64,128]{2,1,0:T(8,128)(2,1)S(1)}, u32[]{:S(2)}, u32[]{:S(2)}) collective-permute-start(bf16[2,64,128]{2,1,0:T(8,128)(2,1)S(1)} %get-tuple-element.42), channel_id=1, source_target_pairs={{32,0},{64,32},{96,64},{128,96},{160,128},{192,160},{224,192},{256... | collective-permute-start | bytes 98312 | tf_op jit(solution)/shard_map/ppermute | solution.py:23
  32.1 7.9 %copy-start.15 = (s32[16,16]{1,0:T(8,128)S(1)}, s32[16,16]{1,0:T(8,128)}, u32[]{:S(2)}) copy-start(s32[16,16]{1,0:T(8,128)} %param.18) | copy-start | bytes 3076
  33.4 6.7 %collective-permute-start.2 = (bf16[18,1,1152]{2,1,0:T(2,128)(2,1)S(1)}, bf16[18,1,1152]{2,1,0:T(2,128)(2,1)S(1)}, u32[]{:S(2)}, u32[]{:S(2)}) collective-permute-start(bf16[18,1,1152]{2,1,0:T(2,128)(2,1)S(1)} %get-tuple-element.31), channel_id=1, source_target_pairs={{0,1},{1,2},{2,3},{3,4},{4,5},{5,6},{6,7},{7,8},{8,9},{9,10},{10,1... | collective-permute-start | bytes 124424 | tf_op jit(solution)/shard_map/ppermute | solution.py:22
  38.1 10.3 %collective-permute-start.3 = (bf16[18,1,1152]{2,1,0:T(2,128)(2,1)S(1)}, bf16[18,1,1152]{2,1,0:T(2,128)(2,1)S(1)}, u32[]{:S(2)}, u32[]{:S(2)}) collective-permute-start(bf16[18,1,1152]{2,1,0:T(2,128)(2,1)S(1)} %get-tuple-element.32), channel_id=1, source_target_pairs={{1,0},{2,1},{3,2},{4,3},{5,4},{6,5},{7,6},{8,7},{9,8},{10,9},{11,1... | collective-permute-start | bytes 124424 | tf_op jit(solution)/shard_map/ppermute | solution.py:23
  49.8 25.7 %copy-start.6 = (bf16[16,16,1152]{2,1,0:T(8,128)(2,1)}, bf16[16,16,1152]{2,1,0:T(8,128)(2,1)S(1)}, u32[]{:S(2)}) copy-start(bf16[16,16,1152]{2,1,0:T(8,128)(2,1)S(1)} %fusion.2) | copy-start | bytes 1769476
  50.1 17.5 %collective-permute-start.8 = (bf16[1,16,128]{2,1,0:T(8,128)(2,1)S(1)}, bf16[1,16,128]{2,1,0:T(8,128)(2,1)S(1)}, u32[]{:S(2)}, u32[]{:S(2)}) collective-permute-start(bf16[1,16,128]{2,1,0:T(8,128)(2,1)S(1)} %get-tuple-element.54), channel_id=1, source_target_pairs={{0,32},{32,64},{64,96},{96,128},{128,160},{160,192},{192,224},{224... | collective-permute-start | bytes 12296 | tf_op jit(solution)/shard_map/ppermute | solution.py:22
  52.0 15.6 %collective-permute-start.9 = (bf16[1,16,128]{2,1,0:T(8,128)(2,1)S(1)}, bf16[1,16,128]{2,1,0:T(8,128)(2,1)S(1)}, u32[]{:S(2)}, u32[]{:S(2)}) collective-permute-start(bf16[1,16,128]{2,1,0:T(8,128)(2,1)S(1)} %get-tuple-element.55), channel_id=1, source_target_pairs={{32,0},{64,32},{96,64},{128,96},{160,128},{192,160},{224,192},{256... | collective-permute-start | bytes 12296 | tf_op jit(solution)/shard_map/ppermute | solution.py:23
  61.8 13.7 %collective-permute-start.6 = (bf16[36,2,128]{2,1,0:T(2,128)(2,1)S(1)}, bf16[36,2,128]{2,1,0:T(2,128)(2,1)S(1)}, u32[]{:S(2)}, u32[]{:S(2)}) collective-permute-start(bf16[36,2,128]{2,1,0:T(2,128)(2,1)S(1)} %get-tuple-element.35), channel_id=1, source_target_pairs={{0,1},{1,2},{2,3},{3,4},{4,5},{5,6},{6,7},{7,8},{8,9},{9,10},{10,1... | collective-permute-start | bytes 55304 | tf_op jit(solution)/shard_map/ppermute | solution.py:22
  63.7 11.8 %collective-permute-start.7 = (bf16[36,2,128]{2,1,0:T(2,128)(2,1)S(1)}, bf16[36,2,128]{2,1,0:T(2,128)(2,1)S(1)}, u32[]{:S(2)}, u32[]{:S(2)}) collective-permute-start(bf16[36,2,128]{2,1,0:T(2,128)(2,1)S(1)} %get-tuple-element.36), channel_id=1, source_target_pairs={{1,0},{2,1},{3,2},{4,3},{5,4},{6,5},{7,6},{8,7},{9,8},{10,9},{11,1... | collective-permute-start | bytes 55304 | tf_op jit(solution)/shard_map/ppermute | solution.py:23
  67.7 8.1 %collective-permute-start.10 = (bf16[18,1,128]{2,1,0:T(2,128)(2,1)S(1)}, bf16[18,1,128]{2,1,0:T(2,128)(2,1)S(1)}, u32[]{:S(2)}, u32[]{:S(2)}) collective-permute-start(bf16[18,1,128]{2,1,0:T(2,128)(2,1)S(1)} %get-tuple-element.43), channel_id=1, source_target_pairs={{0,1},{1,2},{2,3},{3,4},{4,5},{5,6},{6,7},{7,8},{8,9},{9,10},{10,1... | collective-permute-start | bytes 13832 | tf_op jit(solution)/shard_map/ppermute | solution.py:22
  73.5 9.5 %collective-permute-start.11 = (bf16[18,1,128]{2,1,0:T(2,128)(2,1)S(1)}, bf16[18,1,128]{2,1,0:T(2,128)(2,1)S(1)}, u32[]{:S(2)}, u32[]{:S(2)}) collective-permute-start(bf16[18,1,128]{2,1,0:T(2,128)(2,1)S(1)} %get-tuple-element.44), channel_id=1, source_target_pairs={{1,0},{2,1},{3,2},{4,3},{5,4},{6,5},{7,6},{8,7},{9,8},{10,9},{11,1... | collective-permute-start | bytes 13832 | tf_op jit(solution)/shard_map/ppermute | solution.py:23
  113.5 5.5 %copy-start.10 = (f32[32,64]{1,0:T(8,128)S(1)}, f32[32,64]{1,0:T(8,128)}, u32[]{:S(2)}) copy-start(f32[32,64]{1,0:T(8,128)} %param.21) | copy-start | bytes 24580
  121.0 1.0 copy-start.4
  121.0 1.6 copy-start.1
  123.0 11.8 %collective-permute-start.12 = (bf16[2,64,128]{2,1,0:T(8,128)(2,1)S(1)}, bf16[2,64,128]{2,1,0:T(8,128)(2,1)S(1)}, u32[]{:S(2)}, u32[]{:S(2)}) collective-permute-start(bf16[2,64,128]{2,1,0:T(8,128)(2,1)S(1)} %get-tuple-element.39), channel_id=1, source_target_pairs={{0,32},{32,64},{64,96},{96,128},{128,160},{160,192},{192,224},{224... | collective-permute-start | bytes 98312 | tf_op jit(solution)/shard_map/ppermute | solution.py:22
  124.9 11.2 %collective-permute-start.13 = (bf16[2,64,128]{2,1,0:T(8,128)(2,1)S(1)}, bf16[2,64,128]{2,1,0:T(8,128)(2,1)S(1)}, u32[]{:S(2)}, u32[]{:S(2)}) collective-permute-start(bf16[2,64,128]{2,1,0:T(8,128)(2,1)S(1)} %get-tuple-element.40), channel_id=1, source_target_pairs={{32,0},{64,32},{96,64},{128,96},{160,128},{192,160},{224,192},{256... | collective-permute-start | bytes 98312 | tf_op jit(solution)/shard_map/ppermute | solution.py:23
  136.2 6.2 %collective-permute-start.14 = (bf16[36,2,128]{2,1,0:T(2,128)(2,1)S(1)}, bf16[36,2,128]{2,1,0:T(2,128)(2,1)S(1)}, u32[]{:S(2)}, u32[]{:S(2)}) collective-permute-start(bf16[36,2,128]{2,1,0:T(2,128)(2,1)S(1)} %get-tuple-element.33), channel_id=1, source_target_pairs={{0,1},{1,2},{2,3},{3,4},{4,5},{5,6},{6,7},{7,8},{8,9},{9,10},{10,1... | collective-permute-start | bytes 55304 | tf_op jit(solution)/shard_map/ppermute | solution.py:22
  138.1 9.6 %collective-permute-start.15 = (bf16[36,2,128]{2,1,0:T(2,128)(2,1)S(1)}, bf16[36,2,128]{2,1,0:T(2,128)(2,1)S(1)}, u32[]{:S(2)}, u32[]{:S(2)}) collective-permute-start(bf16[36,2,128]{2,1,0:T(2,128)(2,1)S(1)} %get-tuple-element.34), channel_id=1, source_target_pairs={{1,0},{2,1},{3,2},{4,3},{5,4},{6,5},{7,6},{8,7},{9,8},{10,9},{11,1... | collective-permute-start | bytes 55304 | tf_op jit(solution)/shard_map/ppermute | solution.py:23
  150.0 1.2 copy-start.2
  150.0 1.5 copy-start.5
  152.3 13.9 %copy-start.3 = (f32[32,64,128]{2,1,0:T(8,128)}, f32[32,64,128]{2,1,0:T(8,128)S(1)}, u32[]{:S(2)}) copy-start(f32[32,64,128]{2,1,0:T(8,128)S(1)} %fusion.28) | copy-start | bytes 3145732
  153.2 11.6 %collective-permute-start.16 = (f32[2,1,64]{2,1,0:T(1,128)S(1)}, f32[2,1,64]{2,1,0:T(1,128)S(1)}, u32[]{:S(2)}, u32[]{:S(2)}) collective-permute-start(f32[2,1,64]{2,1,0:T(1,128)S(1)} %get-tuple-element.67), channel_id=1, source_target_pairs={{0,32},{32,64},{64,96},{96,128},{128,160},{160,192},{192,224},{224... | collective-permute-start | bytes 1544 | tf_op jit(solution)/shard_map/ppermute | solution.py:22
  155.1 10.9 %collective-permute-start.17 = (f32[2,1,64]{2,1,0:T(1,128)S(1)}, f32[2,1,64]{2,1,0:T(1,128)S(1)}, u32[]{:S(2)}, u32[]{:S(2)}) collective-permute-start(f32[2,1,64]{2,1,0:T(1,128)S(1)} %get-tuple-element.68), channel_id=1, source_target_pairs={{32,0},{64,32},{96,64},{128,96},{160,128},{192,160},{224,192},{256... | collective-permute-start | bytes 1544 | tf_op jit(solution)/shard_map/ppermute | solution.py:23
  166.2 6.0 %collective-permute-start.18 = (f32[2,34,1]{2,1,0:T(8,128)S(1)}, f32[2,34,1]{2,1,0:T(8,128)S(1)}, u32[]{:S(2)}, u32[]{:S(2)}) collective-permute-start(f32[2,34,1]{2,1,0:T(8,128)S(1)} %get-tuple-element.56), channel_id=1, source_target_pairs={{0,1},{1,2},{2,3},{3,4},{4,5},{5,6},{6,7},{7,8},{8,9},{9,10},{10,1... | collective-permute-start | bytes 824 | tf_op jit(solution)/shard_map/ppermute | solution.py:22
  168.1 9.8 %collective-permute-start.19 = (f32[2,34,1]{2,1,0:T(8,128)S(1)}, f32[2,34,1]{2,1,0:T(8,128)S(1)}, u32[]{:S(2)}, u32[]{:S(2)}) collective-permute-start(f32[2,34,1]{2,1,0:T(8,128)S(1)} %get-tuple-element.57), channel_id=1, source_target_pairs={{1,0},{2,1},{3,2},{4,3},{5,4},{6,5},{7,6},{8,7},{9,8},{10,9},{11,1... | collective-permute-start | bytes 824 | tf_op jit(solution)/shard_map/ppermute | solution.py:23
where the time goes:
time: 185 us; the launch traced here: 184 us
  starting transfers between devices  94 us (51%)
  local copies, waits for them, and re-layouts  39.3 us (21%)
  waiting for transfers between devices  29 us (16%)
  other arithmetic  19.9 us (11%)
    ppermute x10, starting transfers between devices, padded_2(): after = lax.ppermute(leading, axis, down)  68 us
    gather x4, local copies, waits for them, and re-layouts, stokes_on(): jnp.take(profiles_flat, slot, axis=0).astype(jnp.float32)  30.3 us
    ppermute x10, waiting for transfers between devices, padded_2(): after = lax.ppermute(leading, axis, down)  29 us
    ppermute x10, starting transfers between devices, padded_2(): before = lax.ppermute(last, axis, up)  26 us
    add x1, other arithmetic, stokes_on(): stokes + normed[:, :, entry:entry + 1] * jnp.take(profiles_flat, slot, ax...  5.47 us
    mul x2, other arithmetic, stencil(): absolute * stokes[:, :, NL:]  4 us
  transfers between devices with their start and end apart: 20, of which 6 were waited for; matrix products, arithmetic and copies ran while one was open for 4% of the time, Pallas kernels for 0%

commit v1 on v0

v1 whole, which is shorter than its diff:
```python
import jax
import jax.numpy as jnp
from jax import lax
from jax.experimental import pallas as pl
from jax.experimental.pallas import tpu as pltpu
from jax.sharding import PartitionSpec as P

NL = 64
LEVELS = 2 * NL
K = 4
RX = 2
RY = 4
PITCH = 32
MESH = pl.DeviceIdType.MESH
F32 = jnp.float32
BF16 = jnp.bfloat16

time_step = 0.5


def kernel(
    size_x,
    size_y,
    spectrum_h,
    courant_h,
    source_h,
    land_h,
    stokes_h,
    velocity_h,
    coriolis_h,
    ocodes_h,
    oweights_h,
    wcodes_h,
    wweights_h,
    spectrum_o,
    velocity_o,
    current_o,
    cells,
    courant,
    source,
    land,
    stokes_kernel,
    wide,
    middle,
    coriolis,
    ocodes,
    oweights,
    wcodes,
    wweights,
    load_sem,
    edge_f,
    edge_s,
    edge_r,
    south_north,
    vx_s,
    vx_r,
    vy_s,
    vy_r,
    mx_s,
    mx_r,
    my_s,
    my_r,
    prof,
    px_s,
    px_r,
    py_s,
    py_r,
    pd_s,
    pd_r,
    select,
    stokes,
    cor,
    coef,
    means,
    ex_s,
    ex_r,
    ey_s,
    ey_r,
    ed_r,
    send_sem,
    recv_sem,
):
    wx, wy, bins = spectrum_o.shape
    ox, oy = velocity_o.shape[:2]
    ix, iy = lax.axis_index("gx"), lax.axis_index("gy")
    at_south, at_north = iy == 0, iy == size_y - 1

    def peer(dx, dy):
        return (lax.rem(ix + dx + size_x, size_x), lax.rem(iy + dy + size_y, size_y))

    straight = ((-1, 0), (1, 0), (0, -1), (0, 1))
    diagonal = ((-1, -1), (-1, 1), (1, -1), (1, 1))
    barrier = pltpu.get_barrier_semaphore()
    for step in straight + diagonal:
        pl.semaphore_signal(barrier, inc=1, device_id=peer(*step), device_id_type=MESH)

    loads = [
        pltpu.make_async_copy(src, dst, load_sem.at[i])
        for i, (src, dst) in enumerate(
            (
                (spectrum_h, cells.at[pl.ds(1, wx)]),
                (velocity_h, wide.at[pl.ds(2, ox), pl.ds(8, oy)]),
                (ocodes_h, ocodes),
                (oweights_h, oweights),
                (coriolis_h, coriolis),
                (wcodes_h, wcodes),
                (wweights_h, wweights),
                (courant_h, courant),
                (source_h, source),
                (land_h, land),
                (stokes_h, stokes_kernel),
            )
        )
    ]
    for load in loads:
        load.start()

    count = [0]

    def remote(src, dst, step):
        i = count[0]
        count[0] += 1
        return pltpu.make_async_remote_copy(
            src_ref=src,
            dst_ref=dst,
            send_sem=send_sem.at[i],
            recv_sem=recv_sem.at[i],
            device_id=peer(*step),
            device_id_type=MESH,
        )

    lane = lax.broadcasted_iota(jnp.int32, (1, LEVELS), 1)
    low = lane < NL

    def swap(value):
        return pltpu.roll(value, NL, 1)

    def pack_x(ref, side, row):
        edge = jnp.where(low, swap(ref[row, pl.ds(8, oy), :]), ref[row + 1, pl.ds(8, oy), :])
        side[...] = edge.astype(BF16)

    def pack_y(ref, side, col):
        edge = jnp.where(low, ref[pl.ds(2, ox), col, :], swap(ref[pl.ds(2, ox), col + 1, :]))
        side[...] = edge.astype(BF16)

    def unpack_x(ref, side, row):
        edge = side[...].astype(F32)
        ref[row, pl.ds(8, oy), :] = swap(edge)
        ref[row + 1, pl.ds(8, oy), :] = edge

    def unpack_y(ref, side, col, outside):
        edge = side[...].astype(F32)
        edge = jnp.where(outside, jnp.zeros_like(edge), edge)
        ref[pl.ds(2, ox), col, :] = edge
        ref[pl.ds(2, ox), col + 1, :] = swap(edge)

    loads[0].wait()
    for x in range(wx):
        row = cells[x + 1].astype(F32)
        edge_f[0, x : x + 1, :] = row[0:1]
        edge_f[1, x : x + 1, :] = row[wy - 1 : wy]
    edge_s[...] = edge_f[...].astype(BF16)
    loads[1].wait()
    pack_x(wide, vx_s.at[0], 2)
    pack_x(wide, vx_s.at[1], ox)
    pack_y(wide, vy_s.at[0], 8)
    pack_y(wide, vy_s.at[1], 6 + oy)

    pl.semaphore_wait(barrier, 8)
    first = [
        remote(cells.at[wx], cells.at[0], (1, 0)),
        remote(cells.at[1], cells.at[wx + 1], (-1, 0)),
        remote(edge_s.at[1], edge_r.at[0], (0, 1)),
        remote(edge_s.at[0], edge_r.at[1], (0, -1)),
        remote(vx_s.at[1], vx_r.at[0], (1, 0)),
        remote(vx_s.at[0], vx_r.at[1], (-1, 0)),
        remote(vy_s.at[1], vy_r.at[0], (0, 1)),
        remote(vy_s.at[0], vy_r.at[1], (0, -1)),
    ]
    for copy in first:
        copy.start()

    for load in loads[2:]:
        load.wait()
    prof[...] = jnp.zeros_like(prof)
    means[...] = jnp.zeros_like(means)
    speed_x, speed_y = courant[0:1, :], courant[1:2, :]
    coef[0:1, :] = 1.0 - jnp.abs(speed_x) - jnp.abs(speed_y)
    coef[1:2, :] = jnp.maximum(speed_x, 0.0)
    coef[2:3, :] = jnp.maximum(-speed_x, 0.0)
    coef[3:4, :] = jnp.maximum(speed_y, 0.0)
    coef[4:5, :] = jnp.maximum(-speed_y, 0.0)

    slot_row = lax.broadcasted_iota(jnp.int32, (LEVELS, LEVELS), 0)
    own_cell = lax.rem(lane, oy) // RY

    @pl.loop(0, wx)
    def _(i):
        def pair(ref, entry):
            return jnp.concatenate(
                [ref[RX * i, entry : entry + 1, :], ref[RX * i + 1, entry : entry + 1, :]], axis=1
            )

        weights = [pair(oweights, entry) for entry in range(K)]
        total = weights[0] + weights[1] + weights[2] + weights[3]
        rows = jnp.zeros((LEVELS, LEVELS), F32)
        for entry in range(K):
            code = pair(ocodes, entry)
            third = lax.shift_right_logical(code * 11, 5)
            slot = third * (PITCH - 3) + code + own_cell
            rows = rows + jnp.where(slot_row == slot, weights[entry] / total, 0.0)
        rows = rows.T
        high = rows.astype(BF16)
        select[i, :, 0:LEVELS] = high
        select[i, :, LEVELS : 2 * LEVELS] = (rows - high.astype(F32)).astype(BF16)

    turned = coriolis[...].T

    @pl.loop(0, ox)
    def _(x):
        here = lax.broadcasted_iota(jnp.int32, (oy, ox), 1) == x
        column = jnp.sum(jnp.where(here, turned, 0.0), axis=1, keepdims=True)
        cor[x] = jnp.broadcast_to(column, (oy, LEVELS))

    for copy in first[:4]:
        copy.wait()
    for side, outside in ((0, at_south), (1, at_north)):
        value = edge_r[side].astype(F32)
        south_north[side] = jnp.where(outside, jnp.zeros_like(value), value)

    growth = land[...].astype(F32)
    gain = (growth * (1.0 + 0.2 * source[...])).T
    damp = (0.1 * growth).T
    chunk = 3 * LEVELS
    cell_y = lax.broadcasted_iota(jnp.int32, (wy, chunk), 0)

    @pl.loop(0, wx)
    def _(x):
        here = lax.broadcasted_iota(jnp.int32, (wy, wx), 1) == x
        gain_x = jnp.sum(jnp.where(here, gain, 0.0), axis=1, keepdims=True)
        damp_x = jnp.sum(jnp.where(here, damp, 0.0), axis=1, keepdims=True)
        for start in range(0, bins, chunk):
            span = pl.ds(start, chunk)
            center = cells[x + 1, :, span].astype(F32)
            south = jnp.where(cell_y == 0, south_north[0, pl.ds(x, 1), span], pltpu.roll(center, 1, 0))
            north = jnp.where(
                cell_y == wy - 1, south_north[1, pl.ds(x, 1), span], pltpu.roll(center, wy - 1, 0)
            )
            advected = (
                coef[0:1, span] * center
                + coef[1:2, span] * cells[x, :, span].astype(F32)
                + coef[2:3, span] * cells[x + 2, :, span].astype(F32)
                + coef[3:4, span] * south
                + coef[4:5, span] * north
            )
            spectrum_o[x, :, span] = (advected * (gain_x - damp_x * advected)).astype(BF16)

    product = jnp.dot(
        spectrum_o[...].reshape(wx * wy, bins), stokes_kernel[...], preferred_element_type=F32
    )
    product = product.astype(BF16).astype(F32)
    product = jnp.where(low, swap(product), -swap(product)).reshape(wx, wy, LEVELS)
    prof[pl.ds(1, wx), pl.ds(1, wy), :] = product

    px_s[0] = product[0].astype(BF16)
    px_s[1] = product[wx - 1].astype(BF16)
    py_s[0] = prof[pl.ds(1, wx), 1, :].astype(BF16)
    py_s[1] = prof[pl.ds(1, wx), wy, :].astype(BF16)
    second = [
        remote(px_s.at[1], px_r.at[0], (1, 0)),
        remote(px_s.at[0], px_r.at[1], (-1, 0)),
        remote(py_s.at[1], py_r.at[0], (0, 1)),
        remote(py_s.at[0], py_r.at[1], (0, -1)),
        remote(px_s.at[1], pd_r.at[0], (1, 1)),
        remote(px_s.at[1], pd_r.at[1], (1, -1)),
        remote(px_s.at[0], pd_r.at[2], (-1, 1)),
        remote(px_s.at[0], pd_r.at[3], (-1, -1)),
    ]
    for copy in second:
        copy.start()
    for copy in first[4:]:
        copy.wait()
    unpack_x(wide, vx_r.at[0], 0)
    unpack_x(wide, vx_r.at[1], ox + 2)
    unpack_y(wide, vy_r.at[0], 6, at_south)
    unpack_y(wide, vy_r.at[1], 8 + oy, at_north)
    for copy in second:
        copy.wait()
    prof[0, pl.ds(1, wy), :] = px_r[0].astype(F32)
    prof[wx + 1, pl.ds(1, wy), :] = px_r[1].astype(F32)
    for side, outside, col in ((0, at_south, 0), (1, at_north, wy + 1)):
        value = py_r[side].astype(F32)
        prof[pl.ds(1, wx), col, :] = jnp.where(outside, jnp.zeros_like(value), value)
    for i, row, col, outside, line in (
        (0, 0, 0, at_south, wy - 1),
        (1, 0, wy + 1, at_north, 0),
        (2, wx + 1, 0, at_south, wy - 1),
        (3, wx + 1, wy + 1, at_north, 0),
    ):
        value = pd_r[i].astype(F32)[line : line + 1]
        prof[row, col : col + 1, :] = jnp.where(outside, jnp.zeros_like(value), value)

    c1 = jnp.where(low, -8.0 / 12.0, 8.0 / 12.0)
    c2 = jnp.where(low, -1.0 / 12.0, 1.0 / 12.0)

    def absolute(ref, x):
        near = jnp.where(low, ref[x + 2, pl.ds(9, oy), :], ref[x + 3, pl.ds(8, oy), :]) - jnp.where(
            low, ref[x + 2, pl.ds(7, oy), :], ref[x + 1, pl.ds(8, oy), :]
        )
        far = jnp.where(low, ref[x + 2, pl.ds(10, oy), :], ref[x + 4, pl.ds(8, oy), :]) - jnp.where(
            low, ref[x + 2, pl.ds(6, oy), :], ref[x, pl.ds(8, oy), :]
        )
        turn = c1 * near - c2 * far
        return cor[x] + turn + swap(turn)

    @pl.loop(0, wx)
    def _(i):
        block = prof[pl.ds(i, 4)].reshape(4 * PITCH, LEVELS).astype(BF16)
        block = jnp.concatenate([block, block], axis=0)
        both = jnp.dot(select[i], block, preferred_element_type=F32)
        for part in range(RX):
            x = RX * i + part
            drift = both[part * oy : (part + 1) * oy]
            stokes[x] = drift
            middle[x + 2, pl.ds(8, oy), :] = (
                wide[x + 2, pl.ds(8, oy), :] + time_step * absolute(wide, x) * drift
            )

    pack_x(middle, mx_s.at[0], 2)
    pack_x(middle, mx_s.at[1], ox)
    pack_y(middle, my_s.at[0], 8)
    pack_y(middle, my_s.at[1], 6 + oy)
    third = [
        remote(mx_s.at[1], mx_r.at[0], (1, 0)),
        remote(mx_s.at[0], mx_r.at[1], (-1, 0)),
        remote(my_s.at[1], my_r.at[0], (0, 1)),
        remote(my_s.at[0], my_r.at[1], (0, -1)),
    ]
    for copy in third:
        copy.start()
    for copy in third:
        copy.wait()
    unpack_x(middle, mx_r.at[0], 0)
    unpack_x(middle, mx_r.at[1], ox + 2)
    unpack_y(middle, my_r.at[0], 6, at_south)
    unpack_y(middle, my_r.at[1], 8 + oy, at_north)

    def finish(x, by_column):
        rate = absolute(middle, x) * stokes[x]
        value = (
            0.5 * (wide[x + 2, pl.ds(8, oy), :] + middle[x + 2, pl.ds(8, oy), :])
            + (0.5 * time_step) * rate
        )
        velocity_o[x] = value
        mean_u = jnp.sum(jnp.where(low, value, 0.0), axis=1, keepdims=True)
        mean_v = jnp.sum(jnp.where(low, 0.0, value), axis=1, keepdims=True)
        by_column = jnp.where(lane == x, mean_u, by_column)
        return jnp.where(lane == x + NL, mean_v, by_column)

    by_column = lax.fori_loop(0, ox, finish, jnp.zeros((oy, LEVELS), F32)) * (1.0 / NL)
    by_row = jnp.concatenate([by_column, jnp.zeros((LEVELS - oy, LEVELS), F32)], axis=0).T
    for c in range(2):
        rows = by_row[c * NL : c * NL + ox]
        means[c, pl.ds(8, ox), :] = rows
        ex_s[0, c : c + 1, :] = rows[0:1]
        ex_s[1, c : c + 1, :] = rows[ox - 1 : ox]
    ey_s[0] = by_column[0:8]
    ey_s[1] = by_column[oy - 8 : oy]
    fourth = [
        remote(ex_s.at[1], ex_r.at[0], (1, 0)),
        remote(ex_s.at[0], ex_r.at[1], (-1, 0)),
        remote(ey_s.at[1], ey_r.at[0], (0, 1)),
        remote(ey_s.at[0], ey_r.at[1], (0, -1)),
        remote(ey_s.at[1], ed_r.at[0], (1, 1)),
        remote(ey_s.at[0], ed_r.at[1], (1, -1)),
        remote(ey_s.at[1], ed_r.at[2], (-1, 1)),
        remote(ey_s.at[0], ed_r.at[3], (-1, -1)),
    ]
    for copy in fourth:
        copy.start()

    target = lax.broadcasted_iota(jnp.int32, (LEVELS, LEVELS), 1)
    origin = lax.broadcasted_iota(jnp.int32, (LEVELS, LEVELS), 0)
    offset = RY * lax.rem(target, wy) + target // wy - 1
    used = lane < (RY + 2) * wy
    spread = jnp.where((origin == (offset & (LEVELS - 1))) & used, 1.0, 0.0)
    repeat = LEVELS // wy
    wave_sum = wweights[:, 0, :] + wweights[:, 1, :] + wweights[:, 2, :] + wweights[:, 3, :]
    tiled = [
        (
            jnp.concatenate([wcodes[:, entry, :]] * repeat, axis=1),
            jnp.concatenate([wweights[:, entry, :] / wave_sum] * repeat, axis=1),
        )
        for entry in range(K)
    ]
    wanted = []
    for a in range(RX + 2):
        number = (RY + 2) * a + lane // wy
        chosen = jnp.zeros((wx, LEVELS), F32)
        for code, weight in tiled:
            chosen = chosen + jnp.where((code == number) & used, weight, 0.0)
        wanted.append(chosen)

    for copy in fourth:
        copy.wait()
    for c in range(2):
        means[c, 7:8, :] = ex_r[0, c : c + 1, :]
        means[c, 8 + ox : 9 + ox, :] = ex_r[1, c : c + 1, :]
    for side, line, outside, spot, near in (
        (0, 7, at_south, LEVELS - 1, (0, 2)),
        (1, 0, at_north, oy, (1, 3)),
    ):
        here = lane == spot
        column = ey_r[side].T[:, line : line + 1]
        for c in range(2):
            inner = column[c * NL : c * NL + ox]
            inner = jnp.where(outside, jnp.zeros_like(inner), inner)
            means[c, pl.ds(8, ox), :] = jnp.where(here, inner, means[c, pl.ds(8, ox), :])
            for index, row, source_x in ((near[0], 7, ox - 1), (near[1], 8 + ox, 0)):
                spot_x = c * NL + source_x
                corner = ed_r[index, line : line + 1, spot_x : spot_x + 1]
                corner = jnp.where(outside, jnp.zeros_like(corner), corner)
                means[c, row : row + 1, :] = jnp.where(here, corner, means[c, row : row + 1, :])

    gathered = jnp.concatenate(
        [means[c, pl.ds(7 + a, wx, stride=RX), :] for a in range(RX + 2) for c in range(2)], axis=0
    )
    gathered = jnp.dot(
        gathered, spread, preferred_element_type=F32, precision=lax.Precision.HIGHEST
    )
    for c in range(2):
        total = jnp.zeros((wx, LEVELS), F32)
        for a in range(RX + 2):
            start = (2 * a + c) * wx
            total = total + gathered[start : start + wx] * wanted[a]
        shift = LEVELS // 2
        while shift >= wy:
            total = total + pltpu.roll(total, shift, 1)
            shift //= 2
        current_o[c] = total[:, :wy]


def solution(mesh):
    size_x, size_y = mesh.shape["gx"], mesh.shape["gy"]

    def step(
        spectrum,
        courant,
        source,
        wave_land,
        stokes_kernel,
        velocity,
        coriolis,
        ocean_codes,
        ocean_weights,
        wave_codes,
        wave_weights,
    ):
        wx, wy, bins = spectrum.shape
        ox, oy, levels = velocity.shape
        turn = lambda value: jnp.transpose(value, (0, 2, 1))
        operands = (
            spectrum,
            courant,
            source,
            wave_land,
            stokes_kernel,
            velocity,
            coriolis,
            turn(ocean_codes),
            turn(ocean_weights),
            turn(wave_codes),
            turn(wave_weights),
        )
        vmem = pltpu.VMEM
        edge_x = vmem((2, oy, levels), BF16)
        edge_y = vmem((2, ox, levels), BF16)
        prof_edge = vmem((2, wx, levels), BF16)
        tile = vmem((2, 8, levels), F32)
        copies = 28
        scratch = [
            vmem((wx + 2, wy, bins), BF16),
            vmem((2, bins), F32),
            vmem((wx, wy), F32),
            vmem((wx, wy), jnp.int32),
            vmem((bins, levels), BF16),
            vmem((ox + 4, oy + 16, levels), F32),
            vmem((ox + 4, oy + 16, levels), F32),
            vmem((ox, oy), F32),
            vmem((ox, K, oy), jnp.int32),
            vmem((ox, K, oy), F32),
            vmem((wx, K, wy), jnp.int32),
            vmem((wx, K, wy), F32),
            pltpu.SemaphoreType.DMA((11,)),
            vmem((2, wx, bins), F32),
            vmem((2, wx, bins), BF16),
            vmem((2, wx, bins), BF16),
            vmem((2, wx, bins), F32),
            edge_x,
            edge_x,
            edge_y,
            edge_y,
            edge_x,
            edge_x,
            edge_y,
            edge_y,
            vmem((wx + 3, PITCH, levels), F32),
            prof_edge,
            prof_edge,
            prof_edge,
            prof_edge,
            prof_edge,
            vmem((4, wx, levels), BF16),
            vmem((wx, levels, 2 * levels), BF16),
            vmem((ox, oy, levels), F32),
            vmem((ox, oy, levels), F32),
            vmem((8, bins), F32),
            vmem((2, ox + 16, levels), F32),
            tile,
            tile,
            tile,
            tile,
            vmem((4, 8, levels), F32),
            pltpu.SemaphoreType.DMA((copies,)),
            pltpu.SemaphoreType.DMA((copies,)),
        ]
        body = lambda *refs: kernel(size_x, size_y, *refs)
        return pl.pallas_call(
            body,
            out_shape=(
                jax.ShapeDtypeStruct((wx, wy, bins), BF16),
                jax.ShapeDtypeStruct((ox, oy, levels), F32),
                jax.ShapeDtypeStruct((2, wx, wy), F32),
            ),
            in_specs=[pl.BlockSpec(memory_space=pltpu.HBM)] * len(operands),
            out_specs=(pl.BlockSpec(memory_space=pltpu.VMEM),) * 3,
            scratch_shapes=scratch,
            compiler_params=pltpu.CompilerParams(
                collective_id=0, has_side_effects=True, vmem_limit_bytes=65000000
            ),
            name="coupled_step",
        )(*operands)

    return jax.shard_map(
        step,
        mesh=mesh,
        in_specs=(
            P("gx", "gy", None),
            P(),
            P("gx", "gy"),
            P("gx", "gy"),
            P(),
            P("gx", "gy", None),
            P("gx", "gy"),
            P("gx", "gy", None),
            P("gx", "gy", None),
            P("gx", "gy", None),
            P("gx", "gy", None),
        ),
        out_specs=(P("gx", "gy", None), P("gx", "gy", None), P(None, "gx", "gy")),
        check_vma=False,
    )
```

time: 185 us -> 57.2 us (0.31)
  the two profiles are of different devices: /device:TPU:216 before, /device:TPU:1 now
where the time goes in v1:
time: 57.2 us; the launch traced here: 57 us
  Pallas kernels  52.8 us (92%)
  local copies, waits for them, and re-layouts  3.59 us (6%)
  between operations  0.65 us (1%)
    pallas_call x1, Pallas kernels, step(): pl.pallas_call(body, out_shape=(jax.ShapeDtypeStruct((wx, wy, bins), BF16...  52.8 us
    unnamed x7, local copies, waits for them, and re-layouts  3.59 us

profile of v1, /device:TPU:1, one launch (start us, length us, event | category | flops | bytes accessed | tf_op | source)
XLA Modules:
  0.0 57.0 jit_solution(7020027492622999496)
XLA Ops:
  0.6 52.8 %coupled_step.1 = (bf16[16,16,1152]{2,1,0:T(8,128)(2,1)}, f32[32,64,128]{2,1,0:T(8,128)}, f32[2,16,16]{2,1,0:T(8,128)}) custom-call(bf16[16,16,1152]{2,1,0:T(8,128)(2,1)} %refs_0_.1, f32[2,1152]{1,0:T(2,128)} %refs_1_.1, f32[16,16]{1,0:T(8,128)} %refs_2_.1, s32[16,16]{1,0:T(8,128)} %refs_3_.1, bf16[1152,128]{1,0:T(8,128)(2,1)} %refs_4_.1, ...), custom_call_target="tpu_custom_call" | custom-call | tf_op jit(solution)/shard_map/coupled_step/pallas_call | solution.py:528
  53.4 0.0 copy-start
  53.4 2.0 %copy.17 = bf16[16,16,1152]{2,1,0:T(8,128)(2,1)} copy(bf16[16,16,1152]{2,1,0:T(8,128)(2,1)} %get-tuple-element.6) | data formatting | bytes 1179648
  55.5 0.0 copy-done
  55.5 0.0 copy-start.1
  55.5 1.0 %copy.18 = f32[32,64,128]{2,1,0:T(8,128)} copy(f32[32,64,128]{2,1,0:T(8,128)S(1)} %copy-done) | data formatting | bytes 2097152
  56.4 0.0 copy-done.1
  56.4 0.6 %copy.19 = f32[2,16,16]{2,1,0:T(8,128)} copy(f32[2,16,16]{2,1,0:T(8,128)S(1)} %copy-done.1) | data formatting | bytes 4096
Async XLA Ops:
  53.4 2.0 %copy-start = (f32[32,64,128]{2,1,0:T(8,128)S(1)}, f32[32,64,128]{2,1,0:T(8,128)}, u32[]{:S(2)}) copy-start(f32[32,64,128]{2,1,0:T(8,128)} %get-tuple-element.7) | copy-start | bytes 3145732
  55.5 1.0 %copy-start.1 = (f32[2,16,16]{2,1,0:T(8,128)S(1)}, f32[2,16,16]{2,1,0:T(8,128)}, u32[]{:S(2)}) copy-start(f32[2,16,16]{2,1,0:T(8,128)} %get-tuple-element.8) | copy-start | bytes 6148

commit v2 on v1

--- a/solution.py
+++ b/solution.py
@@ -60,6 +60,7 @@
     mx_r,
     my_s,
     my_r,
+    strip,
     prof,
     px_s,
     px_r,
@@ -89,9 +90,8 @@
         return (lax.rem(ix + dx + size_x, size_x), lax.rem(iy + dy + size_y, size_y))
 
     straight = ((-1, 0), (1, 0), (0, -1), (0, 1))
-    diagonal = ((-1, -1), (-1, 1), (1, -1), (1, 1))
     barrier = pltpu.get_barrier_semaphore()
-    for step in straight + diagonal:
+    for step in straight:
         pl.semaphore_signal(barrier, inc=1, device_id=peer(*step), device_id_type=MESH)
 
     loads = [
@@ -157,16 +157,17 @@
     loads[0].wait()
     for x in range(wx):
         row = cells[x + 1].astype(F32)
-        edge_f[0, x : x + 1, :] = row[0:1]
-        edge_f[1, x : x + 1, :] = row[wy - 1 : wy]
-    edge_s[...] = edge_f[...].astype(BF16)
+        for slot, col in enumerate((0, 1, wy - 2, wy - 1)):
+            edge_f[slot, x : x + 1, :] = row[col : col + 1]
+    edge_s[0] = edge_f[0].astype(BF16)
+    edge_s[1] = edge_f[3].astype(BF16)
     loads[1].wait()
     pack_x(wide, vx_s.at[0], 2)
     pack_x(wide, vx_s.at[1], ox)
     pack_y(wide, vy_s.at[0], 8)
     pack_y(wide, vy_s.at[1], 6 + oy)
 
-    pl.semaphore_wait(barrier, 8)
+    pl.semaphore_wait(barrier, 4)
     first = [
         remote(cells.at[wx], cells.at[0], (1, 0)),
         remote(cells.at[1], cells.at[wx + 1], (-1, 0)),
@@ -229,13 +230,24 @@
         south_north[side] = jnp.where(outside, jnp.zeros_like(value), value)
 
     growth = land[...].astype(F32)
-    gain = (growth * (1.0 + 0.2 * source[...])).T
-    damp = (0.1 * growth).T
+    gain_rows = growth * (1.0 + 0.2 * source[...])
+    damp_rows = 0.1 * growth
+    gain, damp = gain_rows.T, damp_rows.T
     chunk = 3 * LEVELS
+    cell_x = lax.broadcasted_iota(jnp.int32, (wx, chunk), 0)
     cell_y = lax.broadcasted_iota(jnp.int32, (wy, chunk), 0)
 
-    @pl.loop(0, wx)
-    def _(x):
+    def updated(span, center, west, east, south, north, gain_x, damp_x):
+        advected = (
+            coef[0:1, span] * center
+            + coef[1:2, span] * west
+            + coef[2:3, span] * east
+            + coef[3:4, span] * south
+            + coef[4:5, span] * north
+        )
+        return (advected * (gain_x - damp_x * advected)).astype(BF16)
+
+    def update_row(x):
         here = lax.broadcasted_iota(jnp.int32, (wy, wx), 1) == x
         gain_x = jnp.sum(jnp.where(here, gain, 0.0), axis=1, keepdims=True)
         damp_x = jnp.sum(jnp.where(here, damp, 0.0), axis=1, keepdims=True)
@@ -246,26 +258,37 @@
             north = jnp.where(
                 cell_y == wy - 1, south_north[1, pl.ds(x, 1), span], pltpu.roll(center, wy - 1, 0)
             )
-            advected = (
-                coef[0:1, span] * center
-                + coef[1:2, span] * cells[x, :, span].astype(F32)
-                + coef[2:3, span] * cells[x + 2, :, span].astype(F32)
-                + coef[3:4, span] * south
-                + coef[4:5, span] * north
+            west, east = cells[x, :, span].astype(F32), cells[x + 2, :, span].astype(F32)
+            spectrum_o[x, :, span] = updated(span, center, west, east, south, north, gain_x, damp_x)
+
+    def as_profile(value):
+        value = jnp.dot(value, stokes_kernel[...], preferred_element_type=F32)
+        value = value.astype(BF16).astype(F32)
+        return jnp.where(low, swap(value), -swap(value))
+
+    update_row(0)
+    update_row(wx - 1)
+    strip[0:wx] = spectrum_o[0]
+    strip[wx : 2 * wx] = spectrum_o[wx - 1]
+    for side, col in ((0, 0), (1, wy - 1)):
+        for start in range(0, bins, chunk):
+            span = pl.ds(start, chunk)
+            center = edge_f[3 * side, :, span]
+            before = cells[0, :, span].astype(F32)[col : col + 1]
+            after = cells[wx + 1, :, span].astype(F32)[col : col + 1]
+            west = jnp.where(cell_x == 0, before, pltpu.roll(center, 1, 0))
+            east = jnp.where(cell_x == wx - 1, after, pltpu.roll(center, wx - 1, 0))
+            inner, outer = edge_f[1 + side, :, span], south_north[side, :, span]
+            south, north = (inner, outer) if side else (outer, inner)
+            strip[(2 + side) * wx : (3 + side) * wx, span] = updated(
+                span, center, west, east, south, north,
+                gain_rows[:, col : col + 1], damp_rows[:, col : col + 1],
             )
-            spectrum_o[x, :, span] = (advected * (gain_x - damp_x * advected)).astype(BF16)
-
-    product = jnp.dot(
-        spectrum_o[...].reshape(wx * wy, bins), stokes_kernel[...], preferred_element_type=F32
-    )
-    product = product.astype(BF16).astype(F32)
-    product = jnp.where(low, swap(product), -swap(product)).reshape(wx, wy, LEVELS)
-    prof[pl.ds(1, wx), pl.ds(1, wy), :] = product
-
-    px_s[0] = product[0].astype(BF16)
-    px_s[1] = product[wx - 1].astype(BF16)
-    py_s[0] = prof[pl.ds(1, wx), 1, :].astype(BF16)
-    py_s[1] = prof[pl.ds(1, wx), wy, :].astype(BF16)
+    outermost = as_profile(strip[...]).astype(BF16)
+    px_s[0] = outermost[0:wx]
+    px_s[1] = outermost[wx : 2 * wx]
+    py_s[0] = outermost[2 * wx : 3 * wx]
+    py_s[1] = outermost[3 * wx : 4 * wx]
     second = [
         remote(px_s.at[1], px_r.at[0], (1, 0)),
         remote(px_s.at[0], px_r.at[1], (-1, 0)),
@@ -278,6 +301,13 @@
     ]
     for copy in second:
         copy.start()
+
+    @pl.loop(1, wx - 1)
+    def _(x):
+        update_row(x)
+
+    own = as_profile(spectrum_o[...].reshape(wx * wy, bins))
+    prof[pl.ds(1, wx), pl.ds(1, wy), :] = own.reshape(wx, wy, LEVELS)
     for copy in first[4:]:
         copy.wait()
     unpack_x(wide, vx_r.at[0], 0)
@@ -303,28 +333,40 @@
     c1 = jnp.where(low, -8.0 / 12.0, 8.0 / 12.0)
     c2 = jnp.where(low, -1.0 / 12.0, 1.0 / 12.0)
 
-    def absolute(ref, x):
-        near = jnp.where(low, ref[x + 2, pl.ds(9, oy), :], ref[x + 3, pl.ds(8, oy), :]) - jnp.where(
-            low, ref[x + 2, pl.ds(7, oy), :], ref[x + 1, pl.ds(8, oy), :]
+    def block(ref, x, rows, y, cols):
+        return ref[pl.ds(x + 2, rows), pl.ds(y + 8, cols), :]
+
+    def absolute(ref, x, rows, y, cols):
+        def ahead(step):
+            return jnp.where(
+                low, block(ref, x, rows, y + step, cols), block(ref, x + step, rows, y, cols)
+            )
+
+        turn = c1 * (ahead(1) - ahead(-1)) - c2 * (ahead(2) - ahead(-2))
+        return cor[pl.ds(x, rows), pl.ds(y, cols), :] + turn + pltpu.roll(turn, NL, 2)
+
+    def advance(x, rows, y, cols):
+        drift = stokes[pl.ds(x, rows), pl.ds(y, cols), :]
+        middle[pl.ds(x + 2, rows), pl.ds(y + 8, cols), :] = (
+            block(wide, x, rows, y, cols) + time_step * absolute(wide, x, rows, y, cols) * drift
         )
-        far = jnp.where(low, ref[x + 2, pl.ds(10, oy), :], ref[x + 4, pl.ds(8, oy), :]) - jnp.where(
-            low, ref[x + 2, pl.ds(6, oy), :], ref[x, pl.ds(8, oy), :]
-        )
-        turn = c1 * near - c2 * far
-        return cor[x] + turn + swap(turn)
-
-    @pl.loop(0, wx)
+
+    @pl.loop(0, wx // 2)
+    def _(pair):
+        for part in range(2):
+            i = 2 * pair + part
+            near = prof[pl.ds(i, 4)].reshape(4 * PITCH, LEVELS).astype(BF16)
+            near = jnp.concatenate([near, near], axis=0)
+            both = jnp.dot(select[i], near, preferred_element_type=F32)
+            stokes[pl.ds(RX * i, RX)] = both.reshape(RX, oy, LEVELS)
+
+    advance(0, 2, 0, oy)
+    advance(ox - 2, 2, 0, oy)
+
+    @pl.loop(0, ox // 8)
     def _(i):
-        block = prof[pl.ds(i, 4)].reshape(4 * PITCH, LEVELS).astype(BF16)
-        block = jnp.concatenate([block, block], axis=0)
-        both = jnp.dot(select[i], block, preferred_element_type=F32)
-        for part in range(RX):
-            x = RX * i + part
-            drift = both[part * oy : (part + 1) * oy]
-            stokes[x] = drift
-            middle[x + 2, pl.ds(8, oy), :] = (
-                wide[x + 2, pl.ds(8, oy), :] + time_step * absolute(wide, x) * drift
-            )
+        advance(8 * i, 8, 0, 8)
+        advance(8 * i, 8, oy - 8, 8)
 
     pack_x(middle, mx_s.at[0], 2)
     pack_x(middle, mx_s.at[1], ox)
@@ -338,46 +380,10 @@
     ]
     for copy in third:
         copy.start()
-    for copy in third:
-        copy.wait()
-    unpack_x(middle, mx_r.at[0], 0)
-    unpack_x(middle, mx_r.at[1], ox + 2)
-    unpack_y(middle, my_r.at[0], 6, at_south)
-    unpack_y(middle, my_r.at[1], 8 + oy, at_north)
-
-    def finish(x, by_column):
-        rate = absolute(middle, x) * stokes[x]
-        value = (
-            0.5 * (wide[x + 2, pl.ds(8, oy), :] + middle[x + 2, pl.ds(8, oy), :])
-            + (0.5 * time_step) * rate
-        )
-        velocity_o[x] = value
-        mean_u = jnp.sum(jnp.where(low, value, 0.0), axis=1, keepdims=True)
-        mean_v = jnp.sum(jnp.where(low, 0.0, value), axis=1, keepdims=True)
-        by_column = jnp.where(lane == x, mean_u, by_column)
-        return jnp.where(lane == x + NL, mean_v, by_column)
-
-    by_column = lax.fori_loop(0, ox, finish, jnp.zeros((oy, LEVELS), F32)) * (1.0 / NL)
-    by_row = jnp.concatenate([by_column, jnp.zeros((LEVELS - oy, LEVELS), F32)], axis=0).T
-    for c in range(2):
-        rows = by_row[c * NL : c * NL + ox]
-        means[c, pl.ds(8, ox), :] = rows
-        ex_s[0, c : c + 1, :] = rows[0:1]
-        ex_s[1, c : c + 1, :] = rows[ox - 1 : ox]
-    ey_s[0] = by_column[0:8]
-    ey_s[1] = by_column[oy - 8 : oy]
-    fourth = [
-        remote(ex_s.at[1], ex_r.at[0], (1, 0)),
-        remote(ex_s.at[0], ex_r.at[1], (-1, 0)),
-        remote(ey_s.at[1], ey_r.at[0], (0, 1)),
-        remote(ey_s.at[0], ey_r.at[1], (0, -1)),
-        remote(ey_s.at[1], ed_r.at[0], (1, 1)),
-        remote(ey_s.at[0], ed_r.at[1], (1, -1)),
-        remote(ey_s.at[1], ed_r.at[2], (-1, 1)),
-        remote(ey_s.at[0], ed_r.at[3], (-1, -1)),
-    ]
-    for copy in fourth:
-        copy.start()
+
+    @pl.loop(0, wx)
+    def _(i):
+        advance(RX * i, RX, 8, oy - 16)
 
     target = lax.broadcasted_iota(jnp.int32, (LEVELS, LEVELS), 1)
     origin = lax.broadcasted_iota(jnp.int32, (LEVELS, LEVELS), 0)
@@ -400,6 +406,72 @@
         for code, weight in tiled:
             chosen = chosen + jnp.where((code == number) & used, weight, 0.0)
         wanted.append(chosen)
+
+    for copy in third:
+        copy.wait()
+    unpack_x(middle, mx_r.at[0], 0)
+    unpack_x(middle, mx_r.at[1], ox + 2)
+    unpack_y(middle, my_r.at[0], 6, at_south)
+    unpack_y(middle, my_r.at[1], 8 + oy, at_north)
+
+    def finish(x, rows, y, cols):
+        rate = absolute(middle, x, rows, y, cols) * stokes[pl.ds(x, rows), pl.ds(y, cols), :]
+        old = block(wide, x, rows, y, cols) + block(middle, x, rows, y, cols)
+        value = 0.5 * old + (0.5 * time_step) * rate
+        velocity_o[pl.ds(x, rows), pl.ds(y, cols), :] = value
+        mean_u = jnp.sum(jnp.where(low, value, 0.0), axis=2, keepdims=True)
+        mean_v = jnp.sum(jnp.where(low, 0.0, value), axis=2, keepdims=True)
+        return mean_u * (1.0 / NL), mean_v * (1.0 / NL)
+
+    def finish_into(table, x, rows, y, cols):
+        mean_u, mean_v = finish(x, rows, y, cols)
+        for row in range(rows):
+            table = jnp.where(lane == x + row, mean_u[row], table)
+            table = jnp.where(lane == x + row + NL, mean_v[row], table)
+        return table
+
+    ends = jnp.zeros((oy, LEVELS), F32)
+    for side, x in ((0, 0), (1, ox - 1)):
+        mean_u, mean_v = finish(x, 1, 0, oy)
+        ends = jnp.where(lane == 2 * side, mean_u[0], ends)
+        ends = jnp.where(lane == 2 * side + 1, mean_v[0], ends)
+    ends = jnp.concatenate([ends, jnp.zeros((LEVELS - oy, LEVELS), F32)], axis=0).T
+    ex_s[0, 0:2, :] = ends[0:2]
+    ex_s[1, 0:2, :] = ends[2:4]
+
+    def outer_columns(i, tables):
+        return (
+            finish_into(tables[0], 8 * i, 8, 0, 8),
+            finish_into(tables[1], 8 * i, 8, oy - 8, 8),
+        )
+
+    nothing = jnp.zeros((8, LEVELS), F32)
+    first_cols, last_cols = lax.fori_loop(0, ox // 8, outer_columns, (nothing, nothing))
+    ey_s[0] = first_cols
+    ey_s[1] = last_cols
+    fourth = [
+        remote(ex_s.at[1], ex_r.at[0], (1, 0)),
+        remote(ex_s.at[0], ex_r.at[1], (-1, 0)),
+        remote(ey_s.at[1], ey_r.at[0], (0, 1)),
+        remote(ey_s.at[0], ey_r.at[1], (0, -1)),
+        remote(ey_s.at[1], ed_r.at[0], (1, 1)),
+        remote(ey_s.at[0], ed_r.at[1], (1, -1)),
+        remote(ey_s.at[1], ed_r.at[2], (-1, 1)),
+        remote(ey_s.at[0], ed_r.at[3], (-1, -1)),
+    ]
+    for copy in fourth:
+        copy.start()
+
+    inner_cols = lax.fori_loop(
+        0,
+        wx,
+        lambda i, table: finish_into(table, RX * i, RX, 8, oy - 16),
+        jnp.zeros((oy - 16, LEVELS), F32),
+    )
+    blank = jnp.zeros((LEVELS - oy, LEVELS), F32)
+    by_row = jnp.concatenate([first_cols, inner_cols, last_cols, blank], axis=0).T
+    for c in range(2):
+        means[c, pl.ds(8, ox), :] = by_row[c * NL : c * NL + ox]
 
     for copy in fourth:
         copy.wait()
@@ -492,7 +564,7 @@
             vmem((wx, K, wy), jnp.int32),
             vmem((wx, K, wy), F32),
             pltpu.SemaphoreType.DMA((11,)),
-            vmem((2, wx, bins), F32),
+            vmem((4, wx, bins), F32),
             vmem((2, wx, bins), BF16),
             vmem((2, wx, bins), BF16),
             vmem((2, wx, bins), F32),
@@ -504,6 +576,7 @@
             edge_x,
             edge_y,
             edge_y,
+            vmem((4 * wx, bins), BF16),
             vmem((wx + 3, PITCH, levels), F32),
             prof_edge,
             prof_edge,
@@ -528,18 +601,18 @@
         return pl.pallas_call(
             body,
             out_shape=(
-                jax.ShapeDtypeStruct((wx, wy, bins), BF16),
-                jax.ShapeDtypeStruct((ox, oy, levels), F32),
+                pltpu.VMEM((wx, wy, bins), BF16),
+                pltpu.VMEM((ox, oy, levels), F32),
                 jax.ShapeDtypeStruct((2, wx, wy), F32),
             ),
             in_specs=[pl.BlockSpec(memory_space=pltpu.HBM)] * len(operands),
             out_specs=(pl.BlockSpec(memory_space=pltpu.VMEM),) * 3,
             scratch_shapes=scratch,
             compiler_params=pltpu.CompilerParams(
-                collective_id=0, has_side_effects=True, vmem_limit_bytes=65000000
+                collective_id=0, has_side_effects=True, vmem_limit_bytes=40000000
             ),
             name="coupled_step",
-        )(*operands)
+        )(*[pltpu.with_memory_space_constraint(o, pltpu.HBM) for o in operands])
 
     return jax.shard_map(
         step,

time: 57.2 us -> 48.6 us (0.85)
  Pallas kernels: 52.8 us -> 45.4 us
  local copies, waits for them, and re-layouts: 3.59 us -> 2.39 us
    pallas_call x1, Pallas kernels: 52.8 us -> 45.4 us  [step(): pl.pallas_call(body, out_shape=(pltpu.VMEM((wx, wy, bins), BF16), pltpu.V...]
    unnamed x7 -> x3, local copies, waits for them, and re-layouts: 3.59 us -> 2.39 us
where the time goes in v2:
time: 48.6 us; the launch traced here: 48.4 us
  Pallas kernels  45.4 us (93%)
  local copies, waits for them, and re-layouts  2.39 us (5%)
  between operations  0.64 us (1%)
    pallas_call x1, Pallas kernels, step(): pl.pallas_call(body, out_shape=(pltpu.VMEM((wx, wy, bins), BF16), pltpu.V...  45.4 us
    unnamed x3, local copies, waits for them, and re-layouts  2.39 us

profile of v2, /device:TPU:1, one launch (start us, length us, event | category | flops | bytes accessed | tf_op | source)
XLA Modules:
  0.0 48.4 jit_solution(11674399715394351958)
XLA Ops:
  0.6 45.4 %coupled_step.1 = (bf16[16,16,1152]{2,1,0:T(8,128)(2,1)S(1)}, f32[32,64,128]{2,1,0:T(8,128)S(1)}, f32[2,16,16]{2,1,0:T(8,128)S(1)}) custom-call(bf16[16,16,1152]{2,1,0:T(8,128)(2,1)} %refs_0_.1, f32[2,1152]{1,0:T(2,128)} %refs_1_.1, f32[16,16]{1,0:T(8,128)} %refs_2_.1, s32[16,16]{1,0:T(8,128)} %refs_3_.1, bf16[1152,128]{1,0:T(8,128)(2,1)} %refs_4_.1, ...), custom_call_target="tpu_custom_call" | custom-call | tf_op jit(solution)/shard_map/coupled_step/pallas_call | solution.py:601
  46.0 0.8 %copy.17 = bf16[16,16,1152]{2,1,0:T(8,128)(2,1)} copy(bf16[16,16,1152]{2,1,0:T(8,128)(2,1)S(1)} %get-tuple-element.3) | data formatting | bytes 1179648
  46.8 1.0 %copy.18 = f32[32,64,128]{2,1,0:T(8,128)} copy(f32[32,64,128]{2,1,0:T(8,128)S(1)} %get-tuple-element.4) | data formatting | bytes 2097152
  47.8 0.6 %copy.19 = f32[2,16,16]{2,1,0:T(8,128)} copy(f32[2,16,16]{2,1,0:T(8,128)S(1)} %get-tuple-element.11) | data formatting | bytes 4096

commit v3 on v2

--- a/solution.py
+++ b/solution.py
@@ -178,7 +178,7 @@
         remote(vy_s.at[1], vy_r.at[0], (0, 1)),
         remote(vy_s.at[0], vy_r.at[1], (0, -1)),
     ]
-    for copy in first:
+    for copy in first[:4]:
         copy.start()
 
     for load in loads[2:]:
@@ -299,7 +299,7 @@
         remote(px_s.at[0], pd_r.at[2], (-1, 1)),
         remote(px_s.at[0], pd_r.at[3], (-1, -1)),
     ]
-    for copy in second:
+    for copy in second + first[4:]:
         copy.start()
 
     @pl.loop(1, wx - 1)
@@ -351,10 +351,10 @@
             block(wide, x, rows, y, cols) + time_step * absolute(wide, x, rows, y, cols) * drift
         )
 
-    @pl.loop(0, wx // 2)
-    def _(pair):
-        for part in range(2):
-            i = 2 * pair + part
+    @pl.loop(0, wx // 8)
+    def _(group):
+        for part in range(8):
+            i = 8 * group + part
             near = prof[pl.ds(i, 4)].reshape(4 * PITCH, LEVELS).astype(BF16)
             near = jnp.concatenate([near, near], axis=0)
             both = jnp.dot(select[i], near, preferred_element_type=F32)
@@ -363,10 +363,9 @@
     advance(0, 2, 0, oy)
     advance(ox - 2, 2, 0, oy)
 
-    @pl.loop(0, ox // 8)
-    def _(i):
-        advance(8 * i, 8, 0, 8)
-        advance(8 * i, 8, oy - 8, 8)
+    for i in range(0, ox, 8):
+        advance(i, 8, 0, 8)
+        advance(i, 8, oy - 8, 8)
 
     pack_x(middle, mx_s.at[0], 2)
     pack_x(middle, mx_s.at[1], ox)
@@ -439,14 +438,10 @@
     ex_s[0, 0:2, :] = ends[0:2]
     ex_s[1, 0:2, :] = ends[2:4]
 
-    def outer_columns(i, tables):
-        return (
-            finish_into(tables[0], 8 * i, 8, 0, 8),
-            finish_into(tables[1], 8 * i, 8, oy - 8, 8),
-        )
-
-    nothing = jnp.zeros((8, LEVELS), F32)
-    first_cols, last_cols = lax.fori_loop(0, ox // 8, outer_columns, (nothing, nothing))
+    first_cols = last_cols = jnp.zeros((8, LEVELS), F32)
+    for i in range(0, ox, 8):
+        first_cols = finish_into(first_cols, i, 8, 0, 8)
+        last_cols = finish_into(last_cols, i, 8, oy - 8, 8)
     ey_s[0] = first_cols
     ey_s[1] = last_cols
     fourth = [
@@ -510,6 +505,18 @@
             total = total + pltpu.roll(total, shift, 1)
             shift //= 2
         current_o[c] = total[:, :wy]
+
+
+def store(*refs):
+    sources, targets, sems = refs[:3], refs[3:6], refs[6]
+    copies = [
+        pltpu.make_async_copy(source, target, sems.at[i])
+        for i, (source, target) in enumerate(zip(sources, targets))
+    ]
+    for copy in copies:
+        copy.start()
+    for copy in copies:
+        copy.wait()
 
 
 def solution(mesh):
@@ -598,12 +605,12 @@
             pltpu.SemaphoreType.DMA((copies,)),
         ]
         body = lambda *refs: kernel(size_x, size_y, *refs)
-        return pl.pallas_call(
+        results = pl.pallas_call(
             body,
             out_shape=(
                 pltpu.VMEM((wx, wy, bins), BF16),
                 pltpu.VMEM((ox, oy, levels), F32),
-                jax.ShapeDtypeStruct((2, wx, wy), F32),
+                pltpu.VMEM((2, wx, wy), F32),
             ),
             in_specs=[pl.BlockSpec(memory_space=pltpu.HBM)] * len(operands),
             out_specs=(pl.BlockSpec(memory_space=pltpu.VMEM),) * 3,
@@ -613,6 +620,15 @@
             ),
             name="coupled_step",
         )(*[pltpu.with_memory_space_constraint(o, pltpu.HBM) for o in operands])
+        return pl.pallas_call(
+            store,
+            out_shape=tuple(jax.ShapeDtypeStruct(r.shape, r.dtype) for r in results),
+            in_specs=[pl.BlockSpec(memory_space=pltpu.VMEM)] * 3,
+            out_specs=(pl.BlockSpec(memory_space=pltpu.HBM),) * 3,
+            scratch_shapes=[pltpu.SemaphoreType.DMA((3,))],
+            compiler_params=pltpu.CompilerParams(vmem_limit_bytes=40000000),
+            name="store_results",
+        )(*[pltpu.with_memory_space_constraint(r, pltpu.VMEM) for r in results])
 
     return jax.shard_map(
         step,

time: 48.6 us -> 46.4 us (0.955)
  local copies, waits for them, and re-layouts: 2.39 us -> 0 us
    unnamed x3 -> x0, local copies, waits for them, and re-layouts: 2.39 us -> none
    pallas_call x0 -> x1, Pallas kernels: none -> 1.19 us  [step(): pl.pallas_call(store, out_shape=tuple((jax.ShapeDtypeStruct(r.shape, r.dt...]
    pallas_call x1, Pallas kernels: 45.4 us -> 44.4 us  [step(): pl.pallas_call(body, out_shape=(pltpu.VMEM((wx, wy, bins), BF16), pltpu.V...]
where the time goes in v3:
time: 46.4 us; the launch traced here: 46.2 us
  Pallas kernels  45.6 us (98%)
  between operations  0.64 us (1%)
    pallas_call x1, Pallas kernels, step(): pl.pallas_call(body, out_shape=(pltpu.VMEM((wx, wy, bins), BF16), pltpu.V...  44.4 us
    pallas_call x1, Pallas kernels, step(): pl.pallas_call(store, out_shape=tuple((jax.ShapeDtypeStruct(r.shape, r.dt...  1.19 us

profile of v3, /device:TPU:1, one launch (start us, length us, event | category | flops | bytes accessed | tf_op | source)
XLA Modules:
  0.0 46.2 jit_solution(17797679914652793536)
XLA Ops:
  0.6 44.4 %coupled_step.1 = (bf16[16,16,1152]{2,1,0:T(8,128)(2,1)S(1)}, f32[32,64,128]{2,1,0:T(8,128)S(1)}, f32[2,16,16]{2,1,0:T(8,128)S(1)}) custom-call(bf16[16,16,1152]{2,1,0:T(8,128)(2,1)} %refs_0_.1, f32[2,1152]{1,0:T(2,128)} %refs_1_.1, f32[16,16]{1,0:T(8,128)} %refs_2_.1, s32[16,16]{1,0:T(8,128)} %refs_3_.1, bf16[1152,128]{1,0:T(8,128)(2,1)} %refs_4_.1, ...), custom_call_target="tpu_custom_call" | custom-call | tf_op jit(solution)/shard_map/coupled_step/pallas_call | solution.py:608
  45.0 1.2 %store_results.1 = (bf16[16,16,1152]{2,1,0:T(8,128)(2,1)}, f32[32,64,128]{2,1,0:T(8,128)}, f32[2,16,16]{2,1,0:T(8,128)}) custom-call(bf16[16,16,1152]{2,1,0:T(8,128)(2,1)S(1)} %get-tuple-element.6.refs_0_, f32[32,64,128]{2,1,0:T(8,128)S(1)} %get-tuple-element.7.refs_1_, f32[2,16,16]{2,1,0:T(8,128)S(1)} %get-tuple-element.8.refs_2_), custom_call_target="tpu_custom_call" | custom-call | tf_op jit(solution)/shard_map/store_results/pallas_call | solution.py:623

commit v4 on v3

--- a/solution.py
+++ b/solution.py
@@ -270,6 +270,21 @@
     update_row(wx - 1)
     strip[0:wx] = spectrum_o[0]
     strip[wx : 2 * wx] = spectrum_o[wx - 1]
+    second = [
+        remote(px_s.at[1], px_r.at[0], (1, 0)),
+        remote(px_s.at[0], px_r.at[1], (-1, 0)),
+        remote(py_s.at[1], py_r.at[0], (0, 1)),
+        remote(py_s.at[0], py_r.at[1], (0, -1)),
+        remote(px_s.at[1], pd_r.at[0], (1, 1)),
+        remote(px_s.at[1], pd_r.at[1], (1, -1)),
+        remote(px_s.at[0], pd_r.at[2], (-1, 1)),
+        remote(px_s.at[0], pd_r.at[3], (-1, -1)),
+    ]
+    outermost = as_profile(strip[0 : 2 * wx]).astype(BF16)
+    px_s[0] = outermost[0:wx]
+    px_s[1] = outermost[wx : 2 * wx]
+    for copy in second[4:] + second[:2]:
+        copy.start()
     for side, col in ((0, 0), (1, wy - 1)):
         for start in range(0, bins, chunk):
             span = pl.ds(start, chunk)
@@ -284,22 +299,10 @@
                 span, center, west, east, south, north,
                 gain_rows[:, col : col + 1], damp_rows[:, col : col + 1],
             )
-    outermost = as_profile(strip[...]).astype(BF16)
-    px_s[0] = outermost[0:wx]
-    px_s[1] = outermost[wx : 2 * wx]
-    py_s[0] = outermost[2 * wx : 3 * wx]
-    py_s[1] = outermost[3 * wx : 4 * wx]
-    second = [
-        remote(px_s.at[1], px_r.at[0], (1, 0)),
-        remote(px_s.at[0], px_r.at[1], (-1, 0)),
-        remote(py_s.at[1], py_r.at[0], (0, 1)),
-        remote(py_s.at[0], py_r.at[1], (0, -1)),
-        remote(px_s.at[1], pd_r.at[0], (1, 1)),
-        remote(px_s.at[1], pd_r.at[1], (1, -1)),
-        remote(px_s.at[0], pd_r.at[2], (-1, 1)),
-        remote(px_s.at[0], pd_r.at[3], (-1, -1)),
-    ]
-    for copy in second + first[4:]:
+    outermost = as_profile(strip[2 * wx : 4 * wx]).astype(BF16)
+    py_s[0] = outermost[0:wx]
+    py_s[1] = outermost[wx : 2 * wx]
+    for copy in second[2:4] + first[4:]:
         copy.start()
 
     @pl.loop(1, wx - 1)
@@ -362,27 +365,52 @@
 
     advance(0, 2, 0, oy)
     advance(ox - 2, 2, 0, oy)
-
-    for i in range(0, ox, 8):
-        advance(i, 8, 0, 8)
-        advance(i, 8, oy - 8, 8)
-
     pack_x(middle, mx_s.at[0], 2)
     pack_x(middle, mx_s.at[1], ox)
-    pack_y(middle, my_s.at[0], 8)
-    pack_y(middle, my_s.at[1], 6 + oy)
     third = [
         remote(mx_s.at[1], mx_r.at[0], (1, 0)),
         remote(mx_s.at[0], mx_r.at[1], (-1, 0)),
         remote(my_s.at[1], my_r.at[0], (0, 1)),
         remote(my_s.at[0], my_r.at[1], (0, -1)),
     ]
-    for copy in third:
+    for copy in third[:2]:
+        copy.start()
+
+    for i in range(0, ox, 8):
+        advance(i, 8, 0, 8)
+        advance(i, 8, oy - 8, 8)
+
+    pack_y(middle, my_s.at[0], 8)
+    pack_y(middle, my_s.at[1], 6 + oy)
+    for copy in third[2:]:
         copy.start()
 
     @pl.loop(0, wx)
     def _(i):
         advance(RX * i, RX, 8, oy - 16)
+
+    def finish(x, rows, y, cols):
+        rate = absolute(middle, x, rows, y, cols) * stokes[pl.ds(x, rows), pl.ds(y, cols), :]
+        old = block(wide, x, rows, y, cols) + block(middle, x, rows, y, cols)
+        value = 0.5 * old + (0.5 * time_step) * rate
+        velocity_o[pl.ds(x, rows), pl.ds(y, cols), :] = value
+        mean_u = jnp.sum(jnp.where(low, value, 0.0), axis=2, keepdims=True)
+        mean_v = jnp.sum(jnp.where(low, 0.0, value), axis=2, keepdims=True)
+        return mean_u * (1.0 / NL), mean_v * (1.0 / NL)
+
+    def finish_into(table, x, rows, y, cols):
+        mean_u, mean_v = finish(x, rows, y, cols)
+        for row in range(rows):
+            table = jnp.where(lane == x + row, mean_u[row], table)
+            table = jnp.where(lane == x + row + NL, mean_v[row], table)
+        return table
+
+    inner_cols = lax.fori_loop(
+        1,
+        wx - 1,
+        lambda i, table: finish_into(table, RX * i, RX, 8, oy - 16),
+        jnp.zeros((oy - 16, LEVELS), F32),
+    )
 
     target = lax.broadcasted_iota(jnp.int32, (LEVELS, LEVELS), 1)
     origin = lax.broadcasted_iota(jnp.int32, (LEVELS, LEVELS), 0)
@@ -413,31 +441,6 @@
     unpack_y(middle, my_r.at[0], 6, at_south)
     unpack_y(middle, my_r.at[1], 8 + oy, at_north)
 
-    def finish(x, rows, y, cols):
-        rate = absolute(middle, x, rows, y, cols) * stokes[pl.ds(x, rows), pl.ds(y, cols), :]
-        old = block(wide, x, rows, y, cols) + block(middle, x, rows, y, cols)
-        value = 0.5 * old + (0.5 * time_step) * rate
-        velocity_o[pl.ds(x, rows), pl.ds(y, cols), :] = value
-        mean_u = jnp.sum(jnp.where(low, value, 0.0), axis=2, keepdims=True)
-        mean_v = jnp.sum(jnp.where(low, 0.0, value), axis=2, keepdims=True)
-        return mean_u * (1.0 / NL), mean_v * (1.0 / NL)
-
-    def finish_into(table, x, rows, y, cols):
-        mean_u, mean_v = finish(x, rows, y, cols)
-        for row in range(rows):
-            table = jnp.where(lane == x + row, mean_u[row], table)
-            table = jnp.where(lane == x + row + NL, mean_v[row], table)
-        return table
-
-    ends = jnp.zeros((oy, LEVELS), F32)
-    for side, x in ((0, 0), (1, ox - 1)):
-        mean_u, mean_v = finish(x, 1, 0, oy)
-        ends = jnp.where(lane == 2 * side, mean_u[0], ends)
-        ends = jnp.where(lane == 2 * side + 1, mean_v[0], ends)
-    ends = jnp.concatenate([ends, jnp.zeros((LEVELS - oy, LEVELS), F32)], axis=0).T
-    ex_s[0, 0:2, :] = ends[0:2]
-    ex_s[1, 0:2, :] = ends[2:4]
-
     first_cols = last_cols = jnp.zeros((8, LEVELS), F32)
     for i in range(0, ox, 8):
         first_cols = finish_into(first_cols, i, 8, 0, 8)
@@ -454,15 +457,22 @@
         remote(ey_s.at[1], ed_r.at[2], (-1, 1)),
         remote(ey_s.at[0], ed_r.at[3], (-1, -1)),
     ]
-    for copy in fourth:
-        copy.start()
-
-    inner_cols = lax.fori_loop(
-        0,
-        wx,
-        lambda i, table: finish_into(table, RX * i, RX, 8, oy - 16),
-        jnp.zeros((oy - 16, LEVELS), F32),
-    )
+    for copy in fourth[4:] + fourth[2:4]:
+        copy.start()
+    ends = jnp.zeros((oy, LEVELS), F32)
+    for side, x in ((0, 0), (1, ox - 1)):
+        mean_u, mean_v = finish(x, 1, 0, oy)
+        ends = jnp.where(lane == 2 * side, mean_u[0], ends)
+        ends = jnp.where(lane == 2 * side + 1, mean_v[0], ends)
+    ends = jnp.concatenate([ends, jnp.zeros((LEVELS - oy, LEVELS), F32)], axis=0).T
+    ex_s[0, 0:2, :] = ends[0:2]
+    ex_s[1, 0:2, :] = ends[2:4]
+
+    for copy in fourth[:2]:
+        copy.start()
+
+    inner_cols = finish_into(inner_cols, 0, RX, 8, oy - 16)
+    inner_cols = finish_into(inner_cols, ox - RX, RX, 8, oy - 16)
     blank = jnp.zeros((LEVELS - oy, LEVELS), F32)
     by_row = jnp.concatenate([first_cols, inner_cols, last_cols, blank], axis=0).T
     for c in range(2):

time: 46.4 us -> 45.9 us (0.989)
  Pallas kernels: 45.6 us -> 45.1 us
    pallas_call x1, Pallas kernels: 44.4 us -> 43.9 us  [step(): pl.pallas_call(body, out_shape=(pltpu.VMEM((wx, wy, bins), BF16), pltpu.V...]
where the time goes in v4:
time: 45.9 us; the launch traced here: 45.7 us
  Pallas kernels  45.1 us (98%)
  between operations  0.64 us (1%)
    pallas_call x1, Pallas kernels, step(): pl.pallas_call(body, out_shape=(pltpu.VMEM((wx, wy, bins), BF16), pltpu.V...  43.9 us
    pallas_call x1, Pallas kernels, step(): pl.pallas_call(store, out_shape=tuple((jax.ShapeDtypeStruct(r.shape, r.dt...  1.19 us

profile of v4, /device:TPU:1, one launch (start us, length us, event | category | flops | bytes accessed | tf_op | source)
XLA Modules:
  0.0 45.7 jit_solution(8496677717598209569)
XLA Ops:
  0.6 43.9 %coupled_step.1 = (bf16[16,16,1152]{2,1,0:T(8,128)(2,1)S(1)}, f32[32,64,128]{2,1,0:T(8,128)S(1)}, f32[2,16,16]{2,1,0:T(8,128)S(1)}) custom-call(bf16[16,16,1152]{2,1,0:T(8,128)(2,1)} %refs_0_.1, f32[2,1152]{1,0:T(2,128)} %refs_1_.1, f32[16,16]{1,0:T(8,128)} %refs_2_.1, s32[16,16]{1,0:T(8,128)} %refs_3_.1, bf16[1152,128]{1,0:T(8,128)(2,1)} %refs_4_.1, ...), custom_call_target="tpu_custom_call" | custom-call | tf_op jit(solution)/shard_map/coupled_step/pallas_call | solution.py:618
  44.5 1.2 %store_results.1 = (bf16[16,16,1152]{2,1,0:T(8,128)(2,1)}, f32[32,64,128]{2,1,0:T(8,128)}, f32[2,16,16]{2,1,0:T(8,128)}) custom-call(bf16[16,16,1152]{2,1,0:T(8,128)(2,1)S(1)} %get-tuple-element.6.refs_0_, f32[32,64,128]{2,1,0:T(8,128)S(1)} %get-tuple-element.7.refs_1_, f32[2,16,16]{2,1,0:T(8,128)S(1)} %get-tuple-element.8.refs_2_), custom_call_target="tpu_custom_call" | custom-call | tf_op jit(solution)/shard_map/store_results/pallas_call | solution.py:633

commit v5 on v4

--- a/solution.py
+++ b/solution.py
@@ -195,8 +195,7 @@
     slot_row = lax.broadcasted_iota(jnp.int32, (LEVELS, LEVELS), 0)
     own_cell = lax.rem(lane, oy) // RY
 
-    @pl.loop(0, wx)
-    def _(i):
+    def choose(i):
         def pair(ref, entry):
             return jnp.concatenate(
                 [ref[RX * i, entry : entry + 1, :], ref[RX * i + 1, entry : entry + 1, :]], axis=1
@@ -215,13 +214,10 @@
         select[i, :, 0:LEVELS] = high
         select[i, :, LEVELS : 2 * LEVELS] = (rows - high.astype(F32)).astype(BF16)
 
-    turned = coriolis[...].T
-
-    @pl.loop(0, ox)
-    def _(x):
-        here = lax.broadcasted_iota(jnp.int32, (oy, ox), 1) == x
-        column = jnp.sum(jnp.where(here, turned, 0.0), axis=1, keepdims=True)
-        cor[x] = jnp.broadcast_to(column, (oy, LEVELS))
+    @pl.loop(0, wx // 4)
+    def _(group):
+        for part in range(4):
+            choose(4 * group + part)
 
     for copy in first[:4]:
         copy.wait()
@@ -308,6 +304,16 @@
     @pl.loop(1, wx - 1)
     def _(x):
         update_row(x)
+
+    turned = coriolis[...].T
+
+    @pl.loop(0, ox // 8)
+    def _(group):
+        for part in range(8):
+            x = 8 * group + part
+            here = lax.broadcasted_iota(jnp.int32, (oy, ox), 1) == x
+            column = jnp.sum(jnp.where(here, turned, 0.0), axis=1, keepdims=True)
+            cor[x] = jnp.broadcast_to(column, (oy, LEVELS))
 
     own = as_profile(spectrum_o[...].reshape(wx * wy, bins))
     prof[pl.ds(1, wx), pl.ds(1, wy), :] = own.reshape(wx, wy, LEVELS)

time: 45.9 us -> 45 us (0.980)
  Pallas kernels: 45.1 us -> 44.2 us
    pallas_call x1, Pallas kernels: 43.9 us -> 43 us  [step(): pl.pallas_call(body, out_shape=(pltpu.VMEM((wx, wy, bins), BF16), pltpu.V...]
where the time goes in v5:
time: 45 us; the launch traced here: 44.8 us
  Pallas kernels  44.2 us (98%)
  between operations  0.64 us (1%)
    pallas_call x1, Pallas kernels, step(): pl.pallas_call(body, out_shape=(pltpu.VMEM((wx, wy, bins), BF16), pltpu.V...  43 us
    pallas_call x1, Pallas kernels, step(): pl.pallas_call(store, out_shape=tuple((jax.ShapeDtypeStruct(r.shape, r.dt...  1.19 us

profile of v5, /device:TPU:1, one launch (start us, length us, event | category | flops | bytes accessed | tf_op | source)
XLA Modules:
  0.0 44.8 jit_solution(6818365843325845701)
XLA Ops:
  0.6 43.0 %coupled_step.1 = (bf16[16,16,1152]{2,1,0:T(8,128)(2,1)S(1)}, f32[32,64,128]{2,1,0:T(8,128)S(1)}, f32[2,16,16]{2,1,0:T(8,128)S(1)}) custom-call(bf16[16,16,1152]{2,1,0:T(8,128)(2,1)} %refs_0_.1, f32[2,1152]{1,0:T(2,128)} %refs_1_.1, f32[16,16]{1,0:T(8,128)} %refs_2_.1, s32[16,16]{1,0:T(8,128)} %refs_3_.1, bf16[1152,128]{1,0:T(8,128)(2,1)} %refs_4_.1, ...), custom_call_target="tpu_custom_call" | custom-call | tf_op jit(solution)/shard_map/coupled_step/pallas_call | solution.py:624
  43.6 1.2 %store_results.1 = (bf16[16,16,1152]{2,1,0:T(8,128)(2,1)}, f32[32,64,128]{2,1,0:T(8,128)}, f32[2,16,16]{2,1,0:T(8,128)}) custom-call(bf16[16,16,1152]{2,1,0:T(8,128)(2,1)S(1)} %get-tuple-element.6.refs_0_, f32[32,64,128]{2,1,0:T(8,128)S(1)} %get-tuple-element.7.refs_1_, f32[2,16,16]{2,1,0:T(8,128)S(1)} %get-tuple-element.8.refs_2_), custom_call_target="tpu_custom_call" | custom-call | tf_op jit(solution)/shard_map/store_results/pallas_call | solution.py:639

commit v6 on v5

--- a/solution.py
+++ b/solution.py
@@ -219,16 +219,16 @@
         for part in range(4):
             choose(4 * group + part)
 
+    growth = land[...].astype(F32)
+    gain_rows = growth * (1.0 + 0.2 * source[...])
+    damp_rows = 0.1 * growth
+    gain, damp = gain_rows.T, damp_rows.T
     for copy in first[:4]:
         copy.wait()
     for side, outside in ((0, at_south), (1, at_north)):
         value = edge_r[side].astype(F32)
         south_north[side] = jnp.where(outside, jnp.zeros_like(value), value)
 
-    growth = land[...].astype(F32)
-    gain_rows = growth * (1.0 + 0.2 * source[...])
-    damp_rows = 0.1 * growth
-    gain, damp = gain_rows.T, damp_rows.T
     chunk = 3 * LEVELS
     cell_x = lax.broadcasted_iota(jnp.int32, (wx, chunk), 0)
     cell_y = lax.broadcasted_iota(jnp.int32, (wy, chunk), 0)
@@ -360,15 +360,14 @@
             block(wide, x, rows, y, cols) + time_step * absolute(wide, x, rows, y, cols) * drift
         )
 
-    @pl.loop(0, wx // 8)
-    def _(group):
-        for part in range(8):
-            i = 8 * group + part
-            near = prof[pl.ds(i, 4)].reshape(4 * PITCH, LEVELS).astype(BF16)
-            near = jnp.concatenate([near, near], axis=0)
-            both = jnp.dot(select[i], near, preferred_element_type=F32)
-            stokes[pl.ds(RX * i, RX)] = both.reshape(RX, oy, LEVELS)
-
+    def drift_row(i):
+        near = prof[pl.ds(i, 4)].reshape(4 * PITCH, LEVELS).astype(BF16)
+        near = jnp.concatenate([near, near], axis=0)
+        both = jnp.dot(select[i], near, preferred_element_type=F32)
+        stokes[pl.ds(RX * i, RX)] = both.reshape(RX, oy, LEVELS)
+
+    drift_row(0)
+    drift_row(wx - 1)
     advance(0, 2, 0, oy)
     advance(ox - 2, 2, 0, oy)
     pack_x(middle, mx_s.at[0], 2)
@@ -382,6 +381,8 @@
     for copy in third[:2]:
         copy.start()
 
+    for i in range(1, wx - 1):
+        drift_row(i)
     for i in range(0, ox, 8):
         advance(i, 8, 0, 8)
         advance(i, 8, oy - 8, 8)

time: 45 us -> 44.8 us (level)
  no operation moved by 1% of the time
where the time goes in v6:
time: 44.8 us; the launch traced here: 44.6 us
  Pallas kernels  44 us (98%)
  between operations  0.64 us (1%)
    pallas_call x1, Pallas kernels, step(): pl.pallas_call(body, out_shape=(pltpu.VMEM((wx, wy, bins), BF16), pltpu.V...  42.8 us
    pallas_call x1, Pallas kernels, step(): pl.pallas_call(store, out_shape=tuple((jax.ShapeDtypeStruct(r.shape, r.dt...  1.19 us

profile of v6, /device:TPU:1, one launch (start us, length us, event | category | flops | bytes accessed | tf_op | source)
XLA Modules:
  0.0 44.6 jit_solution(2909325600932665271)
XLA Ops:
  0.6 42.8 %coupled_step.1 = (bf16[16,16,1152]{2,1,0:T(8,128)(2,1)S(1)}, f32[32,64,128]{2,1,0:T(8,128)S(1)}, f32[2,16,16]{2,1,0:T(8,128)S(1)}) custom-call(bf16[16,16,1152]{2,1,0:T(8,128)(2,1)} %refs_0_.1, f32[2,1152]{1,0:T(2,128)} %refs_1_.1, f32[16,16]{1,0:T(8,128)} %refs_2_.1, s32[16,16]{1,0:T(8,128)} %refs_3_.1, bf16[1152,128]{1,0:T(8,128)(2,1)} %refs_4_.1, ...), custom_call_target="tpu_custom_call" | custom-call | tf_op jit(solution)/shard_map/coupled_step/pallas_call | solution.py:625
  43.4 1.2 %store_results.1 = (bf16[16,16,1152]{2,1,0:T(8,128)(2,1)}, f32[32,64,128]{2,1,0:T(8,128)}, f32[2,16,16]{2,1,0:T(8,128)}) custom-call(bf16[16,16,1152]{2,1,0:T(8,128)(2,1)S(1)} %get-tuple-element.6.refs_0_, f32[32,64,128]{2,1,0:T(8,128)S(1)} %get-tuple-element.7.refs_1_, f32[2,16,16]{2,1,0:T(8,128)S(1)} %get-tuple-element.8.refs_2_), custom_call_target="tpu_custom_call" | custom-call | tf_op jit(solution)/shard_map/store_results/pallas_call | solution.py:640

commit v7 on v6

--- a/solution.py
+++ b/solution.py
@@ -301,9 +301,10 @@
     for copy in second[2:4] + first[4:]:
         copy.start()
 
-    @pl.loop(1, wx - 1)
-    def _(x):
-        update_row(x)
+    @pl.loop(0, wx // 2 - 1)
+    def _(group):
+        for part in range(2):
+            update_row(2 * group + part + 1)
 
     turned = coriolis[...].T
 

time: 44.8 us -> 44.8 us (level)
  no operation moved by 1% of the time
where the time goes in v7:
time: 44.8 us; the launch traced here: 44.6 us
  Pallas kernels  44 us (98%)
  between operations  0.64 us (1%)
    pallas_call x1, Pallas kernels, step(): pl.pallas_call(body, out_shape=(pltpu.VMEM((wx, wy, bins), BF16), pltpu.V...  42.8 us
    pallas_call x1, Pallas kernels, step(): pl.pallas_call(store, out_shape=tuple((jax.ShapeDtypeStruct(r.shape, r.dt...  1.19 us

profile of v7, /device:TPU:1, one launch (start us, length us, event | category | flops | bytes accessed | tf_op | source)
XLA Modules:
  0.0 44.6 jit_solution(16896050268580784491)
XLA Ops:
  0.6 42.8 %coupled_step.1 = (bf16[16,16,1152]{2,1,0:T(8,128)(2,1)S(1)}, f32[32,64,128]{2,1,0:T(8,128)S(1)}, f32[2,16,16]{2,1,0:T(8,128)S(1)}) custom-call(bf16[16,16,1152]{2,1,0:T(8,128)(2,1)} %refs_0_.1, f32[2,1152]{1,0:T(2,128)} %refs_1_.1, f32[16,16]{1,0:T(8,128)} %refs_2_.1, s32[16,16]{1,0:T(8,128)} %refs_3_.1, bf16[1152,128]{1,0:T(8,128)(2,1)} %refs_4_.1, ...), custom_call_target="tpu_custom_call" | custom-call | tf_op jit(solution)/shard_map/coupled_step/pallas_call | solution.py:626
  43.4 1.2 %store_results.1 = (bf16[16,16,1152]{2,1,0:T(8,128)(2,1)}, f32[32,64,128]{2,1,0:T(8,128)}, f32[2,16,16]{2,1,0:T(8,128)}) custom-call(bf16[16,16,1152]{2,1,0:T(8,128)(2,1)S(1)} %get-tuple-element.6.refs_0_, f32[32,64,128]{2,1,0:T(8,128)S(1)} %get-tuple-element.7.refs_1_, f32[2,16,16]{2,1,0:T(8,128)S(1)} %get-tuple-element.8.refs_2_), custom_call_target="tpu_custom_call" | custom-call | tf_op jit(solution)/shard_map/store_results/pallas_call | solution.py:641
